TPU v7x, 256 devices: a whole 4x4x8 slice. The times are simulated.
256 devices in a mesh: seq: 32 (over y_lo, z, core), tensor: 8 (over y_hi, x).
Axes of the slice: x: 4, y: 4 (y_hi: 2, y_lo: 2; y = y_hi * 2 + y_lo), z: 8, core: 2. Of those that a mesh axis runs over, the one named last changes fastest.
Arguments:
- features: bfloat16 [4096, 3072], P('seq', 'tensor'), may hold values from -6 to 6
- gain: float32 [3072], replicated, may hold values from 0.1 to 1.9
- w_qkv: bfloat16 [3072, 3, 3072], P(None, None, 'tensor'), may hold values from -0.109375 to 0.109375
- rope_factors: float32 [48], replicated, may hold values from 1 to 64
- cache_len: int32 [4], replicated, may hold values from 1 to 12288, as said below
- cache_kv: bfloat16 [384, 128, 2, 3072], P('seq', None, None, 'tensor'), may hold values from -405 to 405, as said below
- block_owner: int32 [384], P('seq'), may hold values from 0 to 4, as said below
- block_base: int32 [384], P('seq'), may hold values from 0 to 12160, as said below
Outputs:
- attended: bfloat16 [4096, 3072], P('seq', 'tensor')
- new_kv: bfloat16 [4096, 2, 3072], P('seq', None, 'tensor')
Inputs may be any that keep to these rules, and one draw needn't show every extreme that they name: `cache_len`: one request has exactly 12288 cached tokens; the others have between 1 and 9216. `block_owner`: request r owns exactly ceil(cache_len[r] / 128) blocks, placed anywhere in the pool; 4 marks a free block, and some blocks are free. `block_base`: the blocks of request r carry the bases 0, 128, 256, ... below cache_len[r], each once; free blocks carry 0. `cache_kv`: stored keys are already rotated.
All inputs are finite; a program needn't handle non-finite values.
Results may differ from a plain program's by a relative error of at most 0.014.
The roundings to bfloat16 on the way count: a program that leaves them out, or rounds other values in their place, can miss the bound.
Values may be sent and summed in bfloat16 or wider, within the bound.
No kernel may reach another device: no remote copies, remote signals or barrier semaphores. Data moves between devices by JAX's collectives and lax.ppermute only.
A program may use at most 384 MiB of HBM per device.

v0:
```python
import functools

import jax
import jax.numpy as jnp
from jax import lax
from jax.experimental import pallas as pl
from jax.experimental.pallas import tpu as pltpu
from jax.sharding import Mesh, PartitionSpec as P


S = jax.ShapeDtypeStruct
EPSILON = 1e-05
NEG = -1e30
FLOOR = -1e29
MSCALE = 1.1902380714238083
F32 = jnp.float32
BF = jnp.bfloat16
I32 = jnp.int32
VM = pl.BlockSpec(memory_space=pltpu.VMEM)
SM = pl.BlockSpec(memory_space=pltpu.SMEM)
HBM = pl.BlockSpec(memory_space=pl.ANY)
HD = 96
HALF = 6
WIN = ((0,), (0, 1), (1, 2), (2,))
DIST = (4, 3, 5, 2, 6, 1, 7)


def ring(n, k):
    return [(i, (i + k) % n) for i in range(n)]


def pick(first):
    i = lax.broadcasted_iota(I32, (128, 256), 0)
    j = lax.broadcasted_iota(I32, (128, 256), 1)
    return (j == 2 * i + first).astype(F32).astype(BF)


def prep_body(kv_ref, o_ref):
    x = kv_ref[...].reshape(256, 384)
    k = jnp.dot(pick(0), x, preferred_element_type=F32).astype(BF)
    v = jnp.dot(pick(1), x, preferred_element_type=F32)
    for t in range(3):
        o_ref[128 * t:128 * t + 128] = k[:, 128 * t:128 * t + 128]
    o_ref[384:768] = v.T.astype(BF)


def prep(kv, first):
    return pl.pallas_call(
        prep_body,
        grid=(HALF,),
        in_specs=[pl.BlockSpec((None, 128, 2, 384), lambda i: (i + first, 0, 0, 0))],
        out_specs=pl.BlockSpec((None, 768, 128), lambda i: (i, 0, 0)),
        out_shape=S((HALF, 768, 128), BF),
        name="prep",
    )(kv)


def rotate(t, cos, sin):
    out = []
    for h in range(4):
        a = t[HD * h:HD * h + 48]
        b = t[HD * h + 48:HD * h + 96]
        out.append(a * cos - b * sin)
        out.append(b * cos + a * sin)
    return jnp.concatenate(out, axis=0)


def chunk_ids():
    yh = lax.axis_index("yh")
    x = lax.axis_index("x")
    ids = []
    for dx in (0, 3, 1, 2):
        xs = lax.rem(x + dx, 4)
        ids += [yh * 4 + xs, (1 - yh) * 4 + xs]
    return ids


def query_body(gain_ref, cos_ref, sin_ref, f0, f1, fr, fl, fm, w_hbm, q_ref, n_ref, wbuf, sem):
    ids = chunk_ids()
    copies = []
    for j in range(8):
        rows = pl.ds(pl.multiple_of(ids[j] * 384, 384), 384)
        c = pltpu.make_async_copy(w_hbm.at[0, rows], wbuf.at[j], sem.at[j])
        c.start()
        copies.append(c)
    chunks = [f0[...], f1[...]]
    for f in (fr, fl, fm):
        chunks += [f[0:128], f[128:256]]
    wide = [c.astype(F32) for c in chunks]
    total = jnp.zeros((128, 384), F32)
    for x in wide:
        total = total + x * x
    scale = lax.rsqrt(jnp.sum(total, axis=1, keepdims=True) * (1.0 / 3072) + EPSILON)
    acc = jnp.zeros((128, 384), F32)
    for j in range(8):
        n = (wide[j] * scale * gain_ref[ids[j]]).astype(BF)
        n_ref[j] = n
        copies[j].wait()
        acc = acc + jnp.dot(n, wbuf[j], preferred_element_type=F32)
    q_ref[...] = (rotate(acc.T, cos_ref[...], sin_ref[...]) * HD ** (-0.5)).astype(BF)


def keyval_body(cos_ref, sin_ref, n_ref, w_hbm, new_ref, k_ref, v_ref, wbuf, sem):
    ids = chunk_ids()
    copies = []
    for c in range(2):
        for j in range(8):
            rows = pl.ds(pl.multiple_of(ids[j] * 384, 384), 384)
            d = pltpu.make_async_copy(w_hbm.at[1 + c, rows], wbuf.at[c, j], sem.at[c, j])
            d.start()
            copies.append(d)
    accs = []
    for c in range(2):
        acc = jnp.zeros((128, 384), F32)
        for j in range(8):
            copies[8 * c + j].wait()
            acc = acc + jnp.dot(n_ref[j], wbuf[c, j], preferred_element_type=F32)
        accs.append(acc)
    k = rotate(accs[0].T, cos_ref[...], sin_ref[...]).T.astype(BF)
    v = accs[1]
    k_ref[...] = k
    v_ref[...] = v.astype(BF)
    for t in range(3):
        new_ref[128 * t:128 * t + 128] = k[:, 128 * t:128 * t + 128]
    new_ref[384:768] = v.T.astype(BF)


def attn_body(sets, has_new, has_prev, *refs):
    len_ref, *refs = refs
    metas, refs = refs[:4], refs[4:]
    q_refs, refs = refs[:8], refs[8:]
    kv_refs, refs = refs[:len(sets)], refs[len(sets):]
    new_refs, refs = (refs[:2], refs[2:]) if has_new else ((), refs)
    prev_refs, refs = (refs[:8], refs[8:]) if has_prev else ((), refs)
    out_refs, refs = refs[:8], refs[8:]
    kv, qa, oa, qm, s_ref, acc, idx, cnt, val, sem = refs
    nc = HALF * len(sets)
    z = lax.axis_index("z")
    core = lax.axis_index("c")
    req0 = 2 * lax.axis_index("yl")
    nreq = lax.div(z, 4)
    npos = [(lax.rem(z, 4) * 2 + core) * 128, (lax.rem(z, 4) * 2 + 1 - core) * 128]
    for i, ref in enumerate(new_refs):
        pltpu.make_async_copy(ref, kv.at[nc + i], sem.at[nc + i]).start()
    for r in range(2):
        cnt[r] = 0
        idx[r, 0] = 0
    uses = []
    for i, (m, first) in enumerate(sets):
        for b in range(HALF):
            j = HALF * i + b
            o = metas[m][0, first + b] - req0
            use = (o >= 0) & (o < 2)
            uses.append(use)

            @pl.when(use)
            def _():
                pltpu.make_async_copy(kv_refs[i].at[b], kv.at[j], sem.at[j]).start()
                val[j] = jnp.clip(len_ref[o + req0] - metas[m][1, first + b], 0, 128)
                c = cnt[o]
                idx[o, c] = j
                cnt[o] = c + 1

    for d in range(8):
        qa[lax.rem(z + d, 8)] = q_refs[d][...]
        if has_prev:
            oa[lax.rem(z + d, 8)] = prev_refs[d][...]
    for i, ref in enumerate(new_refs):
        pltpu.make_async_copy(ref, kv.at[nc + i], sem.at[nc + i]).wait()
    for i, (m, first) in enumerate(sets):
        for b in range(HALF):
            j = HALF * i + b

            @pl.when(uses[j])
            def _():
                pltpu.make_async_copy(kv_refs[i].at[b], kv.at[j], sem.at[j]).wait()

    ii = lax.broadcasted_iota(I32, (128, 256), 0)
    lane = lax.broadcasted_iota(I32, (1, 256), 1)
    hrow = lax.broadcasted_iota(I32, (384, 256), 0)

    def pair(pr, carry):
        r = lax.div(pr, 2)
        start = lax.rem(pr, 2) * 512 + core * 128
        tp = start + jnp.where(lane < 128, lane, lane + 128)
        q = jnp.concatenate([qa[2 * pr], qa[2 * pr + 1]], axis=1)
        for h in range(4):
            for w, t in enumerate(WIN[h]):
                rr = hrow[128 * t:128 * t + 128]
                sel = (rr >= HD * h) & (rr < HD * h + HD)
                block = q[128 * t:128 * t + 128].astype(F32)
                qm[h, 128 * w:128 * w + 128] = jnp.where(sel, block, 0.0).astype(BF)
        cached = cnt[r]
        for i in range(len(new_refs)):
            @pl.when((nreq == r) & (npos[i] <= start + 256))
            def _():
                c = cnt[r]
                idx[r, c] = nc + i
                cnt[r] = c + 1
        n = cnt[r]
        cnt[r] = cached
        idx[r, n] = idx[r, 0]
        steps = lax.div(n + 1, 2)

        def entry(k):
            j = idx[r, k]
            live = k < n
            isn = live & (j >= nc)
            np_ = jnp.where(j == nc, npos[0], npos[1])
            v = jnp.where(live & (j < nc), val[jnp.minimum(j, nc - 1)], 0)
            full = jnp.where(isn, start - np_ >= 127, v >= 128)
            return j, isn, np_, v, full

        def scores(g, m):
            e = [entry(2 * g), entry(2 * g + 1)]
            mm = []
            for h in range(4):
                rows = [
                    jnp.concatenate([kv[x[0], 128 * t:128 * t + 128] for t in WIN[h]], axis=1)
                    for x in e
                ]
                lhs = jnp.concatenate(rows, axis=0)
                s = jnp.dot(lhs, qm[h, 0:128 * len(WIN[h])], preferred_element_type=F32)
                s_ref[g, h] = s
                mm.append(jnp.maximum(m[h], jnp.max(s.reshape(32, 8, 256), axis=0)))

            def masked():
                out = []
                for h in range(4):
                    top = m[h]
                    for x in range(2):
                        _, isn, np_, v, _ = e[x]
                        thr = jnp.where(isn, tp - np_, v - 1)
                        s = jnp.where(ii <= thr, s_ref[g, h, 128 * x:128 * x + 128], NEG)
                        s_ref[g, h, 128 * x:128 * x + 128] = s
                        top = jnp.maximum(top, jnp.max(s.reshape(16, 8, 256), axis=0))
                    out.append(top)
                return tuple(out)

            return lax.cond(e[0][4] & e[1][4], lambda: tuple(mm), masked)

        m = lax.fori_loop(0, steps, scores, tuple(jnp.full((8, 256), NEG, F32) for _ in range(4)))
        mx = [jnp.maximum(jnp.max(m[h], axis=0, keepdims=True), FLOOR) for h in range(4)]
        acc[...] = jnp.zeros_like(acc)

        def weigh(g, l):
            j0 = idx[r, 2 * g]
            j1 = idx[r, 2 * g + 1]
            nl = []
            for h in range(4):
                w = jnp.exp(s_ref[g, h] - mx[h])
                nl.append(l[h] + jnp.sum(w.reshape(32, 8, 256), axis=0))
                at = slice(384 + HD * h, 384 + HD * h + HD)
                vt = jnp.concatenate([kv[j0, at], kv[j1, at]], axis=1)
                acc[h] += jnp.dot(vt, w.astype(BF), preferred_element_type=F32)
            return tuple(nl)

        l = lax.fori_loop(0, steps, weigh, tuple(jnp.zeros((8, 256), F32) for _ in range(4)))
        terms = [[], [], []]
        if has_prev:
            old = jnp.concatenate([oa[2 * pr, 384:400], oa[2 * pr + 1, 384:400]], axis=1).astype(F32)
            old = old[0:4] + old[4:8] + old[8:12]
        for h in range(4):
            at = slice(HD * h, HD * h + HD)
            total = jnp.sum(l[h], axis=0, keepdims=True)
            has = total > 0
            safe = jnp.where(has, total, 1.0)
            lse = jnp.where(has, mx[h] + jnp.log(safe), NEG)
            inv = 1.0 / safe
            if has_prev:
                top = jnp.maximum(lse, old[h:h + 1])
                w_new = jnp.exp(lse - top)
                w_old = jnp.exp(old[h:h + 1] - top)
                both = w_new + w_old
                lse = top + jnp.log(both)
                before = jnp.concatenate([oa[2 * pr, at], oa[2 * pr + 1, at]], axis=1).astype(F32)
                o = acc[h] * (inv * w_new / both) + before * (w_old / both)
            else:
                o = acc[h] * inv
            o = o.astype(BF)
            oa[2 * pr, at] = o[:, :128]
            oa[2 * pr + 1, at] = o[:, 128:]
            for term in terms:
                part = lse.astype(BF).astype(F32)
                term.append(part)
                lse = lse - part
        rows = terms[0] + terms[1] + terms[2] + [jnp.zeros((4, 256), F32)]
        st = jnp.concatenate(rows, axis=0).astype(BF)
        oa[2 * pr, 384:400] = st[:, :128]
        oa[2 * pr + 1, 384:400] = st[:, 128:]
        return carry

    lax.fori_loop(0, 4, pair, 0)
    for d in range(8):
        out_refs[d][...] = oa[lax.rem(z + d, 8)]


def attn(sets, lens, metas, qs, kvs, news=(), prev=()):
    nb = HALF * len(sets) + 2
    return pl.pallas_call(
        functools.partial(attn_body, sets, bool(news), bool(prev)),
        in_specs=[SM] * 5 + [VM] * 8 + [HBM] * (len(kvs) + len(news)) + [VM] * len(prev),
        out_specs=[VM] * 8,
        out_shape=[S((400, 128), BF)] * 8,
        scratch_shapes=[
            pltpu.VMEM((nb, 768, 128), BF),
            pltpu.VMEM((8, 384, 128), BF),
            pltpu.VMEM((8, 400, 128), BF),
            pltpu.VMEM((4, 256, 256), BF),
            pltpu.VMEM((nb // 2, 4, 256, 256), F32),
            pltpu.VMEM((4, HD, 256), F32),
            pltpu.SMEM((2, nb + 1), I32),
            pltpu.SMEM((2,), I32),
            pltpu.SMEM((nb,), I32),
            pltpu.SemaphoreType.DMA((nb,)),
        ],
        name="attn",
    )(lens, *metas, *qs, *kvs, *news, *prev)


def combine_body(*refs):
    o_ref = refs[-1]
    parts = refs[:-1]
    lses = []
    for p in parts:
        st = p[384:400].astype(F32)
        lses.append(st[0:4] + st[4:8] + st[8:12])
    top = functools.reduce(jnp.maximum, lses)
    ws = [jnp.exp(x - top) for x in lses]
    inv = 1.0 / functools.reduce(jnp.add, ws)
    ws = [w * inv for w in ws]
    rows = []
    for h in range(4):
        acc = jnp.zeros((HD, 128), F32)
        for p, w in zip(parts, ws):
            acc = acc + p[HD * h:HD * h + HD].astype(F32) * w[h:h + 1]
        rows.append(acc)
    o_ref[...] = jnp.concatenate(rows, axis=0).T.astype(BF)


def layer(features, gain, w_qkv, rope_factors, cache_len, cache_kv, block_owner, block_base):
    swap = ring(2, 1)

    f1 = lax.ppermute(features, "yh", swap)
    kv0a = prep(cache_kv, 0)
    kv2a = lax.ppermute(kv0a, "yl", swap)
    both = jnp.concatenate([features, f1], axis=0)
    fm = lax.ppermute(both, "x", ring(4, 2))
    fr = lax.ppermute(both, "x", ring(4, 1))
    fl = lax.ppermute(both, "x", ring(4, -1))

    kv0b = prep(cache_kv, HALF)
    kv2b = lax.ppermute(kv0b, "yl", swap)
    kv1a = lax.ppermute(kv0a, "c", swap)
    kv1b = lax.ppermute(kv0b, "c", swap)
    kv3a = lax.ppermute(kv2a, "c", swap)
    kv3b = lax.ppermute(kv2b, "c", swap)
    meta = jnp.stack([block_owner, block_base])
    m2 = lax.ppermute(meta, "yl", swap)
    m1 = lax.ppermute(meta, "c", swap)
    m3 = lax.ppermute(m2, "c", swap)
    metas = [meta, m1, m2, m3]

    z = lax.axis_index("z")
    request = 2 * lax.axis_index("yl") + z // 4
    start = ((z % 4) * 2 + lax.axis_index("c")) * 128
    positions = cache_len[request] + start + jnp.arange(128, dtype=I32)
    inv_freq = 1.0 / (rope_factors * jnp.power(10000.0, jnp.arange(48, dtype=F32) * 2.0 / HD))
    angles = inv_freq[:, None] * positions.astype(F32)[None, :]
    cos = jnp.cos(angles) * MSCALE
    sin = jnp.sin(angles) * MSCALE

    w = w_qkv.transpose(1, 0, 2)
    q, normed = pl.pallas_call(
        query_body,
        in_specs=[VM] * 8 + [HBM],
        out_specs=[VM, VM],
        out_shape=[S((384, 128), BF), S((8, 128, 384), BF)],
        scratch_shapes=[pltpu.VMEM((8, 384, 384), BF), pltpu.SemaphoreType.DMA((8,))],
        name="query",
    )(gain.reshape(8, 1, 384), cos, sin, features, f1, fr, fl, fm, w)
    qs = [q] + [None] * 7
    for d in DIST:
        qs[d] = lax.ppermute(q, "z", ring(8, -d))
    new0, kn, vn = pl.pallas_call(
        keyval_body,
        in_specs=[VM] * 3 + [HBM],
        out_specs=[VM, VM, VM],
        out_shape=[S((768, 128), BF), S((128, 384), BF), S((128, 384), BF)],
        scratch_shapes=[pltpu.VMEM((2, 8, 384, 384), BF), pltpu.SemaphoreType.DMA((2, 8))],
        name="keyval",
    )(cos, sin, normed, w)
    new_kv = jnp.stack([kn, vn], axis=1)
    new1 = lax.ppermute(new0, "c", swap)
    sets = ((0, 0), (0, HALF), (1, 0), (1, HALF), (2, 0), (3, 0))
    parts = attn(sets, cache_len, metas, qs, [kv0a, kv0b, kv1a, kv1b, kv2a, kv3a], [new0, new1])
    sets = ((2, HALF), (3, HALF))
    parts = attn(sets, cache_len, metas, qs, [kv2b, kv3b], prev=parts)
    got = [parts[0]]
    for d in DIST:
        got.append(lax.ppermute(parts[d], "z", ring(8, d)))
    attended = pl.pallas_call(
        combine_body,
        in_specs=[VM] * 8,
        out_specs=VM,
        out_shape=S((128, 384), BF),
        name="combine",
    )(*got)
    return attended, new_kv


def solution(mesh):
    wide = Mesh(mesh.devices.reshape(2, 8, 2, 2, 4), ("yl", "z", "c", "yh", "x"))
    seq = ("yl", "z", "c")
    ten = ("yh", "x")
    in_specs = (
        P(seq, ten),
        P(),
        P(None, None, ten),
        P(),
        P(),
        P(seq, None, None, ten),
        P(seq),
        P(seq),
    )
    out_specs = (P(seq, ten), P(seq, None, ten))
    return jax.shard_map(layer, mesh=wide, in_specs=in_specs, out_specs=out_specs, check_vma=False)
```

profile of v0, /device:TPU:2, one launch (start us, length us, event | category | flops | bytes accessed | tf_op | source)
XLA Modules:
  0.0 198.4 jit_solution(7570087674712629204)
XLA Ops:
  0.6 5.2 %prep.3.refs_13_ = bf16[6,768,128]{2,1,0:T(8,128)(2,1)} custom-call(bf16[12,128,2,384]{3,2,1,0:T(2,128)(2,1)} %kv_ref.3), custom_call_target="tpu_custom_call" | custom-call | tf_op jit(solution)/shard_map/prep/pallas_call | solution.py:48
  5.9 0.0 copy-start.20
  5.9 1.7 collective-permute-start.18
  7.6 5.2 %prep.2.refs_14_ = bf16[6,768,128]{2,1,0:T(8,128)(2,1)} custom-call(bf16[12,128,2,384]{3,2,1,0:T(2,128)(2,1)} %kv_ref.3), custom_call_target="tpu_custom_call" | custom-call | tf_op jit(solution)/shard_map/prep/pallas_call | solution.py:48
  12.8 0.4 collective-permute-start.14
  13.3 3.2 %collective-permute-start.3 = (bf16[128,384]{1,0:T(8,128)(2,1)S(1)}, bf16[128,384]{1,0:T(8,128)(2,1)S(1)}, u32[]{:S(2)}, u32[]{:S(2)}) collective-permute-start(bf16[128,384]{1,0:T(8,128)(2,1)S(1)} %copy-done.3), channel_id=1, source_target_pairs={{0,4},{4,0},{1,5},{5,1},{2,6},{6,2},{3,7},{7,3},{8,12},{12,8},{9,1... | collective-permute-start | bytes 294920 | tf_op jit(solution)/shard_map/ppermute | solution.py:344
  16.5 0.8 collective-permute-start.1
  17.2 0.7 constant_dynamic-update-slice_fusion.1
  17.9 45.9 %collective-permute-done.3.f1 = bf16[128,384]{1,0:T(8,128)(2,1)S(1)} collective-permute-done((bf16[128,384]{1,0:T(8,128)(2,1)S(1)}, bf16[128,384]{1,0:T(8,128)(2,1)S(1)}, u32[]{:S(2)}, u32[]{:S(2)}) %collective-permute-start.3) | collective-permute-done | bytes 98336 | tf_op jit(solution)/shard_map/ppermute | solution.py:344
  63.8 0.6 copy-done.4
  64.4 0.7 constant_dynamic-update-slice_fusion
  65.1 1.5 collective-permute-start.4
  66.5 0.5 collective-permute-start.5
  67.1 0.6 dynamic_slice.3
  67.8 0.0 collective-permute-done.1.refs_3_
  67.8 0.0 collective-permute-start
  68.4 0.5 collective-permute-done.refs_2_
  69.0 0.2 collective-permute-start.16
  69.1 1.8 collective-permute-done.4.fr
  70.9 0.0 collective-permute-start.17
  70.9 0.0 collective-permute-done.18.refs_17_
  70.9 0.5 collective-permute-start.19
  71.4 0.2 copy-done.5
  71.6 0.0 collective-permute-done.14.refs_13_
  71.6 0.0 collective-permute-start.15
  71.6 0.9 collective-permute-done.5.fl
  72.5 2.3 %collective-permute-start.6 = (bf16[256,384]{1,0:T(8,128)(2,1)}, bf16[256,384]{1,0:T(8,128)(2,1)}, u32[]{:S(2)}, u32[]{:S(2)}) collective-permute-start(bf16[256,384]{1,0:T(8,128)(2,1)} %constant_dynamic-update-slice_fusion), channel_id=1, source_target_pairs={{0,2},{1,3},{2,0},{3,1},{4,6},{5,7},{6,4},{7,5},{8,10},{9,11},{10,... | collective-permute-start | bytes 589832 | tf_op jit(solution)/shard_map/ppermute | solution.py:348
  74.9 0.8 fusion.1
  75.6 5.1 %collective-permute-done.6.fm = bf16[256,384]{1,0:T(8,128)(2,1)} collective-permute-done((bf16[256,384]{1,0:T(8,128)(2,1)}, bf16[256,384]{1,0:T(8,128)(2,1)}, u32[]{:S(2)}, u32[]{:S(2)}) %collective-permute-start.6) | collective-permute-done | bytes 196640 | tf_op jit(solution)/shard_map/ppermute | solution.py:348
  80.8 0.0 collective-permute-start.2
  80.8 4.6 %query.1 = (bf16[384,128]{1,0:T(8,128)(2,1)}, bf16[8,128,384]{2,1,0:T(8,128)(2,1)}) custom-call(f32[8,1,384]{2,1,0:T(1,128)} %bitcast.11, f32[48,128]{1,0:T(8,128)} %get-tuple-element.47.cos_ref, f32[48,128]{1,0:T(8,128)} %get-tuple-element.46.sin_ref, bf16[128,384]{1,0:T(8,128)(2,1)} %f0.1, bf16[128,384]{1,0:T(8,128)(2,1)} %copy-done.4, ...), custom_call_target="tpu_custom_call" | custom-call | tf_op jit(solution)/shard_map/query/pallas_call | solution.py:374
  85.4 0.0 collective-permute-done.2.refs_4_
  85.4 7.3 %collective-permute-start.10 = (bf16[384,128]{1,0:T(8,128)(2,1)}, bf16[384,128]{1,0:T(8,128)(2,1)}, u32[]{:S(2)}, u32[]{:S(2)}) collective-permute-start(bf16[384,128]{1,0:T(8,128)(2,1)} %get-tuple-element.23.refs_5_), channel_id=1, source_target_pairs={{0,64},{16,80},{32,96},{48,112},{64,0},{80,16},{96,32},{112,48},{1... | collective-permute-start | bytes 294920 | tf_op jit(solution)/shard_map/ppermute | solution.py:384
  92.7 3.9 %collective-permute-done.10.refs_9_ = bf16[384,128]{1,0:T(8,128)(2,1)} collective-permute-done((bf16[384,128]{1,0:T(8,128)(2,1)}, bf16[384,128]{1,0:T(8,128)(2,1)}, u32[]{:S(2)}, u32[]{:S(2)}) %collective-permute-start.10) | collective-permute-done | bytes 98336 | tf_op jit(solution)/shard_map/ppermute | solution.py:384
  96.6 3.0 %collective-permute-start.11 = (bf16[384,128]{1,0:T(8,128)(2,1)}, bf16[384,128]{1,0:T(8,128)(2,1)}, u32[]{:S(2)}, u32[]{:S(2)}) collective-permute-start(bf16[384,128]{1,0:T(8,128)(2,1)} %get-tuple-element.23.refs_5_), channel_id=1, source_target_pairs={{0,48},{16,64},{32,80},{48,96},{64,112},{80,0},{96,16},{112,32},{1... | collective-permute-start | bytes 294920 | tf_op jit(solution)/shard_map/ppermute | solution.py:384
  99.6 9.3 %collective-permute-done.11.refs_10_ = bf16[384,128]{1,0:T(8,128)(2,1)} collective-permute-done((bf16[384,128]{1,0:T(8,128)(2,1)}, bf16[384,128]{1,0:T(8,128)(2,1)}, u32[]{:S(2)}, u32[]{:S(2)}) %collective-permute-start.11) | collective-permute-done | bytes 98336 | tf_op jit(solution)/shard_map/ppermute | solution.py:384
  108.9 1.4 collective-permute-start.12
  110.3 7.8 %collective-permute-done.12.refs_11_ = bf16[384,128]{1,0:T(8,128)(2,1)} collective-permute-done((bf16[384,128]{1,0:T(8,128)(2,1)}, bf16[384,128]{1,0:T(8,128)(2,1)}, u32[]{:S(2)}, u32[]{:S(2)}) %collective-permute-start.12) | collective-permute-done | bytes 98336 | tf_op jit(solution)/shard_map/ppermute | solution.py:384
  118.1 1.9 collective-permute-start.13
  119.9 4.3 %collective-permute-done.13.refs_12_ = bf16[384,128]{1,0:T(8,128)(2,1)} collective-permute-done((bf16[384,128]{1,0:T(8,128)(2,1)}, bf16[384,128]{1,0:T(8,128)(2,1)}, u32[]{:S(2)}, u32[]{:S(2)}) %collective-permute-start.13) | collective-permute-done | bytes 98336 | tf_op jit(solution)/shard_map/ppermute | solution.py:384
  124.2 1.0 collective-permute-start.7
  125.2 3.9 %collective-permute-done.7.refs_6_ = bf16[384,128]{1,0:T(8,128)(2,1)} collective-permute-done((bf16[384,128]{1,0:T(8,128)(2,1)}, bf16[384,128]{1,0:T(8,128)(2,1)}, u32[]{:S(2)}, u32[]{:S(2)}) %collective-permute-start.7) | collective-permute-done | bytes 98336 | tf_op jit(solution)/shard_map/ppermute | solution.py:384
  129.2 2.4 %collective-permute-start.8 = (bf16[384,128]{1,0:T(8,128)(2,1)}, bf16[384,128]{1,0:T(8,128)(2,1)}, u32[]{:S(2)}, u32[]{:S(2)}) collective-permute-start(bf16[384,128]{1,0:T(8,128)(2,1)} %get-tuple-element.23.refs_5_), channel_id=1, source_target_pairs={{0,96},{16,112},{32,0},{48,16},{64,32},{80,48},{96,64},{112,80},{1... | collective-permute-start | bytes 294920 | tf_op jit(solution)/shard_map/ppermute | solution.py:384
  131.5 4.3 %collective-permute-done.8.refs_7_ = bf16[384,128]{1,0:T(8,128)(2,1)} collective-permute-done((bf16[384,128]{1,0:T(8,128)(2,1)}, bf16[384,128]{1,0:T(8,128)(2,1)}, u32[]{:S(2)}, u32[]{:S(2)}) %collective-permute-start.8) | collective-permute-done | bytes 98336 | tf_op jit(solution)/shard_map/ppermute | solution.py:384
  135.8 1.2 collective-permute-start.9
  137.1 6.0 %keyval.1 = (bf16[768,128]{1,0:T(8,128)(2,1)}, bf16[128,384]{1,0:T(8,128)(2,1)}, bf16[128,384]{1,0:T(8,128)(2,1)}) custom-call(f32[48,128]{1,0:T(8,128)} %get-tuple-element.47.cos_ref, f32[48,128]{1,0:T(8,128)} %get-tuple-element.46.sin_ref, bf16[8,128,384]{2,1,0:T(8,128)(2,1)} %get-tuple-element.24.n_ref, bf16[3,3072,384]{2,1,0:T(8,128)(2,1)} %bitcast.8), custom_call_target="tpu_custom_call" | custom-call | tf_op jit(solution)/shard_map/keyval/pallas_call | solution.py:385
  143.1 0.1 collective-permute-start.20
  143.2 1.6 collective-permute-done.20.refs_20_
  144.8 0.0 collective-permute-done.16.refs_15_
  144.9 0.7 copy-done.6
  145.6 9.8 %attn.2 = (bf16[400,128]{1,0:T(8,128)(2,1)}, bf16[400,128]{1,0:T(8,128)(2,1)}, bf16[400,128]{1,0:T(8,128)(2,1)}, bf16[400,128]{1,0:T(8,128)(2,1)}, bf16[400,128]...) custom-call(s32[4]{0:T(128)} %refs_0_.3, s32[2,12]{1,0:T(2,128)} %copy-done.16, ...), custom_call_target="tpu_custom_call" | custom-call | tf_op jit(solution)/shard_map/attn/pallas_call | solution.py:300
  155.4 1.0 copy-done.2
  156.4 7.0 %attn.3 = (bf16[400,128]{1,0:T(8,128)(2,1)}, bf16[400,128]{1,0:T(8,128)(2,1)}, bf16[400,128]{1,0:T(8,128)(2,1)}, bf16[400,128]{1,0:T(8,128)(2,1)}, bf16[400,128]...) custom-call(s32[4]{0:T(128)} %refs_0_.3, s32[2,12]{1,0:T(2,128)} %copy-done.16, ...), custom_call_target="tpu_custom_call" | custom-call | tf_op jit(solution)/shard_map/attn/pallas_call | solution.py:300
  163.4 6.6 %collective-permute-start.21 = (bf16[400,128]{1,0:T(8,128)(2,1)}, bf16[400,128]{1,0:T(8,128)(2,1)S(1)}, u32[]{:S(2)}, u32[]{:S(2)}) collective-permute-start(bf16[400,128]{1,0:T(8,128)(2,1)} %get-tuple-element.35), channel_id=1, source_target_pairs={{0,64},{16,80},{32,96},{48,112},{64,0},{80,16},{96,32},{112,48},{1... | collective-permute-start | bytes 307208 | tf_op jit(solution)/shard_map/ppermute | solution.py:401
  170.0 5.8 %collective-permute-start.22 = (bf16[400,128]{1,0:T(8,128)(2,1)}, bf16[400,128]{1,0:T(8,128)(2,1)S(1)}, u32[]{:S(2)}, u32[]{:S(2)}) collective-permute-start(bf16[400,128]{1,0:T(8,128)(2,1)} %get-tuple-element.36), channel_id=1, source_target_pairs={{0,48},{16,64},{32,80},{48,96},{64,112},{80,0},{96,16},{112,32},{1... | collective-permute-start | bytes 307208 | tf_op jit(solution)/shard_map/ppermute | solution.py:401
  175.8 6.8 %collective-permute-start.24 = (bf16[400,128]{1,0:T(8,128)(2,1)}, bf16[400,128]{1,0:T(8,128)(2,1)S(1)}, u32[]{:S(2)}, u32[]{:S(2)}) collective-permute-start(bf16[400,128]{1,0:T(8,128)(2,1)} %get-tuple-element.38), channel_id=1, source_target_pairs={{0,32},{16,48},{32,64},{48,80},{64,96},{80,112},{96,0},{112,16},{1... | collective-permute-start | bytes 307208 | tf_op jit(solution)/shard_map/ppermute | solution.py:401
  182.6 0.0 collective-permute-start.25
  182.6 1.1 collective-permute-start.26
  183.7 0.3 collective-permute-done.22.refs_2_
  184.0 9.1 %collective-permute-start.27 = (bf16[400,128]{1,0:T(8,128)(2,1)}, bf16[400,128]{1,0:T(8,128)(2,1)S(1)}, u32[]{:S(2)}, u32[]{:S(2)}) collective-permute-start(bf16[400,128]{1,0:T(8,128)(2,1)} %get-tuple-element.41), channel_id=1, source_target_pairs={{0,112},{16,0},{32,16},{48,32},{64,48},{80,64},{96,80},{112,96},{1... | collective-permute-start | bytes 307208 | tf_op jit(solution)/shard_map/ppermute | solution.py:401
  193.1 0.9 copy.10
  194.1 1.6 collective-permute-done.27.refs_7_
  195.7 0.6 copy-done.13
  196.3 2.1 %combine.1 = bf16[128,384]{1,0:T(8,128)(2,1)} custom-call(bf16[400,128]{1,0:T(8,128)(2,1)} %get-tuple-element.34.refs_0_, bf16[400,128]{1,0:T(8,128)(2,1)} %copy-done.7, bf16[400,128]{1,0:T(8,128)(2,1)} %copy-done.8, bf16[400,128]{1,0:T(8,128)(2,1)} %copy-done.9, bf16[400,128]{1,0:T(8,128)(2,1)} %copy-done.10, bf16[400,128]{1,0:T(8,128)(2,1)} %copy-done.11, ...), custom_call_target="tpu_custom_call" | custom-call | tf_op jit(solution)/shard_map/combine/pallas_call | solution.py:402
  (56 shorter events, 0.2 us)
Async XLA Ops:
  5.9 7.4 %copy-start.3 = (bf16[128,384]{1,0:T(8,128)(2,1)S(1)}, bf16[128,384]{1,0:T(8,128)(2,1)}, u32[]{:S(2)}) copy-start(bf16[128,384]{1,0:T(8,128)(2,1)} %f0.1) | copy-start | bytes 294916
  5.9 10.6 %copy-start.21 = (s32[12]{0:T(128)S(1)}, s32[12]{0:T(128)}, u32[]{:S(2)}) copy-start(s32[12]{0:T(128)} %param.15) | copy-start | bytes 148
  5.9 10.6 %copy-start.22 = (s32[12]{0:T(128)S(1)}, s32[12]{0:T(128)}, u32[]{:S(2)}) copy-start(s32[12]{0:T(128)} %param.14) | copy-start | bytes 148
  5.9 61.2 %copy-start.23 = (f32[48]{0:T(128)S(1)}, f32[48]{0:T(128)}, u32[]{:S(2)}) copy-start(f32[48]{0:T(128)} %param.11) | copy-start | bytes 580
  5.9 61.2 %copy-start.20 = (s32[4]{0:T(128)S(1)}, s32[4]{0:T(128)}, u32[]{:S(2)}) copy-start(s32[4]{0:T(128)} %refs_0_.3) | copy-start | bytes 52
  5.9 63.1 %copy-start = (bf16[6,768,128]{2,1,0:T(8,128)(2,1)S(1)}, bf16[6,768,128]{2,1,0:T(8,128)(2,1)}, u32[]{:S(2)}) copy-start(bf16[6,768,128]{2,1,0:T(8,128)(2,1)} %prep.3.refs_13_) | copy-start | bytes 3538948
  5.9 65.0 %collective-permute-start.18 = (bf16[6,768,128]{2,1,0:T(8,128)(2,1)}, bf16[6,768,128]{2,1,0:T(8,128)(2,1)}, u32[]{:S(2)}, u32[]{:S(2)}) collective-permute-start(bf16[6,768,128]{2,1,0:T(8,128)(2,1)} %prep.3.refs_13_), channel_id=1, source_target_pairs={{0,128},{128,0},{1,129},{129,1},{2,130},{130,2},{3,131},{131,3},{4... | collective-permute-start | bytes 3538952 | tf_op jit(solution)/shard_map/ppermute | solution.py:346
  12.8 58.8 %collective-permute-start.14 = (bf16[6,768,128]{2,1,0:T(8,128)(2,1)}, bf16[6,768,128]{2,1,0:T(8,128)(2,1)S(1)}, u32[]{:S(2)}, u32[]{:S(2)}) collective-permute-start(bf16[6,768,128]{2,1,0:T(8,128)(2,1)} %prep.2.refs_14_), channel_id=1, source_target_pairs={{0,128},{128,0},{1,129},{129,1},{2,130},{130,2},{3,131},{131,3},{4... | collective-permute-start | bytes 3538952 | tf_op jit(solution)/shard_map/ppermute | solution.py:353
  13.3 50.5 %collective-permute-start.3 = (bf16[128,384]{1,0:T(8,128)(2,1)S(1)}, bf16[128,384]{1,0:T(8,128)(2,1)S(1)}, u32[]{:S(2)}, u32[]{:S(2)}) collective-permute-start(bf16[128,384]{1,0:T(8,128)(2,1)S(1)} %copy-done.3), channel_id=1, source_target_pairs={{0,4},{4,0},{1,5},{5,1},{2,6},{6,2},{3,7},{7,3},{8,12},{12,8},{9,1... | collective-permute-start | bytes 294920 | tf_op jit(solution)/shard_map/ppermute | solution.py:344
  16.5 68.9 %copy-start.16 = (s32[2,12]{1,0:T(2,128)}, s32[2,12]{1,0:T(2,128)S(1)}, u32[]{:S(2)}) copy-start(s32[2,12]{1,0:T(2,128)S(1)} %pad_add_fusion.refs_1_) | copy-start | bytes 292
  16.5 51.3 %collective-permute-start.1 = (s32[2,12]{1,0:T(2,128)S(1)}, s32[2,12]{1,0:T(2,128)S(1)}, u32[]{:S(2)}, u32[]{:S(2)}) collective-permute-start(s32[2,12]{1,0:T(2,128)S(1)} %pad_add_fusion.refs_1_), channel_id=1, source_target_pairs={{0,128},{128,0},{1,129},{129,1},{2,130},{130,2},{3,131},{131,3},{4... | collective-permute-start | bytes 296 | tf_op jit(solution)/shard_map/ppermute | solution.py:359
  63.8 0.6 copy-start.4
  65.1 5.9 %collective-permute-start.4 = (bf16[256,384]{1,0:T(8,128)(2,1)}, bf16[256,384]{1,0:T(8,128)(2,1)S(1)}, u32[]{:S(2)}, u32[]{:S(2)}) collective-permute-start(bf16[256,384]{1,0:T(8,128)(2,1)} %constant_dynamic-update-slice_fusion), channel_id=1, source_target_pairs={{0,1},{1,2},{2,3},{3,0},{4,5},{5,6},{6,7},{7,4},{8,9},{9,10},{10,1... | collective-permute-start | bytes 589832 | tf_op jit(solution)/shard_map/ppermute | solution.py:349
  66.5 6.0 %collective-permute-start.5 = (bf16[256,384]{1,0:T(8,128)(2,1)}, bf16[256,384]{1,0:T(8,128)(2,1)}, u32[]{:S(2)}, u32[]{:S(2)}) collective-permute-start(bf16[256,384]{1,0:T(8,128)(2,1)} %constant_dynamic-update-slice_fusion), channel_id=1, source_target_pairs={{0,3},{1,0},{2,1},{3,2},{4,7},{5,4},{6,5},{7,6},{8,11},{9,8},{10,9... | collective-permute-start | bytes 589832 | tf_op jit(solution)/shard_map/ppermute | solution.py:350
  67.8 17.6 %copy-start.17 = (s32[2,12]{1,0:T(2,128)}, s32[2,12]{1,0:T(2,128)S(1)}, u32[]{:S(2)}) copy-start(s32[2,12]{1,0:T(2,128)S(1)} %collective-permute-done.1.refs_3_) | copy-start | bytes 292
  67.8 1.2 collective-permute-start
  69.0 16.4 %copy-start.18 = (s32[2,12]{1,0:T(2,128)}, s32[2,12]{1,0:T(2,128)S(1)}, u32[]{:S(2)}) copy-start(s32[2,12]{1,0:T(2,128)S(1)} %collective-permute-done.refs_2_) | copy-start | bytes 292
  69.0 75.9 %collective-permute-start.16 = (bf16[6,768,128]{2,1,0:T(8,128)(2,1)S(1)}, bf16[6,768,128]{2,1,0:T(8,128)(2,1)}, u32[]{:S(2)}, u32[]{:S(2)}) collective-permute-start(bf16[6,768,128]{2,1,0:T(8,128)(2,1)S(1)} %copy-done), channel_id=1, source_target_pairs={{0,8},{8,0},{1,9},{9,1},{2,10},{10,2},{3,11},{11,3},{4,12},{12,4},... | collective-permute-start | bytes 3538952 | tf_op jit(solution)/shard_map/ppermute | solution.py:354
  70.9 0.7 copy-start.5
  70.9 74.6 %collective-permute-start.17 = (bf16[6,768,128]{2,1,0:T(8,128)(2,1)}, bf16[6,768,128]{2,1,0:T(8,128)(2,1)}, u32[]{:S(2)}, u32[]{:S(2)}) collective-permute-start(bf16[6,768,128]{2,1,0:T(8,128)(2,1)} %prep.2.refs_14_), channel_id=1, source_target_pairs={{0,8},{8,0},{1,9},{9,1},{2,10},{10,2},{3,11},{11,3},{4,12},{12,4},... | collective-permute-start | bytes 3538952 | tf_op jit(solution)/shard_map/ppermute | solution.py:355
  70.9 74.6 %collective-permute-start.19 = (bf16[6,768,128]{2,1,0:T(8,128)(2,1)}, bf16[6,768,128]{2,1,0:T(8,128)(2,1)}, u32[]{:S(2)}, u32[]{:S(2)}) collective-permute-start(bf16[6,768,128]{2,1,0:T(8,128)(2,1)} %collective-permute-done.18.refs_17_), channel_id=1, source_target_pairs={{0,8},{8,0},{1,9},{9,1},{2,10},{10,2},{3,11},{11,3},{4,12},{12,4},... | collective-permute-start | bytes 3538952 | tf_op jit(solution)/shard_map/ppermute | solution.py:356
  71.6 13.7 %copy-start.1 = (bf16[6,768,128]{2,1,0:T(8,128)(2,1)}, bf16[6,768,128]{2,1,0:T(8,128)(2,1)S(1)}, u32[]{:S(2)}) copy-start(bf16[6,768,128]{2,1,0:T(8,128)(2,1)S(1)} %collective-permute-done.14.refs_13_) | copy-start | bytes 3538948
  71.6 83.8 %collective-permute-start.15 = (bf16[6,768,128]{2,1,0:T(8,128)(2,1)S(1)}, bf16[6,768,128]{2,1,0:T(8,128)(2,1)S(1)}, u32[]{:S(2)}, u32[]{:S(2)}) collective-permute-start(bf16[6,768,128]{2,1,0:T(8,128)(2,1)S(1)} %collective-permute-done.14.refs_13_), channel_id=1, source_target_pairs={{0,8},{8,0},{1,9},{9,1},{2,10},{10,2},{3,11},{11,3},{4,12},{12,4},... | collective-permute-start | bytes 3538952 | tf_op jit(solution)/shard_map/ppermute | solution.py:357
  72.5 8.2 %collective-permute-start.6 = (bf16[256,384]{1,0:T(8,128)(2,1)}, bf16[256,384]{1,0:T(8,128)(2,1)}, u32[]{:S(2)}, u32[]{:S(2)}) collective-permute-start(bf16[256,384]{1,0:T(8,128)(2,1)} %constant_dynamic-update-slice_fusion), channel_id=1, source_target_pairs={{0,2},{1,3},{2,0},{3,1},{4,6},{5,7},{6,4},{7,5},{8,10},{9,11},{10,... | collective-permute-start | bytes 589832 | tf_op jit(solution)/shard_map/ppermute | solution.py:348
  80.8 4.6 %collective-permute-start.2 = (s32[2,12]{1,0:T(2,128)S(1)}, s32[2,12]{1,0:T(2,128)S(1)}, u32[]{:S(2)}, u32[]{:S(2)}) collective-permute-start(s32[2,12]{1,0:T(2,128)S(1)} %collective-permute-done.1.refs_3_), channel_id=1, source_target_pairs={{0,8},{8,0},{1,9},{9,1},{2,10},{10,2},{3,11},{11,3},{4,12},{12,4},... | collective-permute-start | bytes 296 | tf_op jit(solution)/shard_map/ppermute | solution.py:361
  85.4 57.7 %copy-start.19 = (s32[2,12]{1,0:T(2,128)}, s32[2,12]{1,0:T(2,128)S(1)}, u32[]{:S(2)}) copy-start(s32[2,12]{1,0:T(2,128)S(1)} %collective-permute-done.2.refs_4_) | copy-start | bytes 292
  85.4 11.2 %collective-permute-start.10 = (bf16[384,128]{1,0:T(8,128)(2,1)}, bf16[384,128]{1,0:T(8,128)(2,1)}, u32[]{:S(2)}, u32[]{:S(2)}) collective-permute-start(bf16[384,128]{1,0:T(8,128)(2,1)} %get-tuple-element.23.refs_5_), channel_id=1, source_target_pairs={{0,64},{16,80},{32,96},{48,112},{64,0},{80,16},{96,32},{112,48},{1... | collective-permute-start | bytes 294920 | tf_op jit(solution)/shard_map/ppermute | solution.py:384
  96.6 12.3 %collective-permute-start.11 = (bf16[384,128]{1,0:T(8,128)(2,1)}, bf16[384,128]{1,0:T(8,128)(2,1)}, u32[]{:S(2)}, u32[]{:S(2)}) collective-permute-start(bf16[384,128]{1,0:T(8,128)(2,1)} %get-tuple-element.23.refs_5_), channel_id=1, source_target_pairs={{0,48},{16,64},{32,80},{48,96},{64,112},{80,0},{96,16},{112,32},{1... | collective-permute-start | bytes 294920 | tf_op jit(solution)/shard_map/ppermute | solution.py:384
  108.9 9.2 %collective-permute-start.12 = (bf16[384,128]{1,0:T(8,128)(2,1)}, bf16[384,128]{1,0:T(8,128)(2,1)}, u32[]{:S(2)}, u32[]{:S(2)}) collective-permute-start(bf16[384,128]{1,0:T(8,128)(2,1)} %get-tuple-element.23.refs_5_), channel_id=1, source_target_pairs={{0,32},{16,48},{32,64},{48,80},{64,96},{80,112},{96,0},{112,16},{1... | collective-permute-start | bytes 294920 | tf_op jit(solution)/shard_map/ppermute | solution.py:384
  118.1 6.1 %collective-permute-start.13 = (bf16[384,128]{1,0:T(8,128)(2,1)}, bf16[384,128]{1,0:T(8,128)(2,1)}, u32[]{:S(2)}, u32[]{:S(2)}) collective-permute-start(bf16[384,128]{1,0:T(8,128)(2,1)} %get-tuple-element.23.refs_5_), channel_id=1, source_target_pairs={{0,16},{16,32},{32,48},{48,64},{64,80},{80,96},{96,112},{112,0},{1... | collective-permute-start | bytes 294920 | tf_op jit(solution)/shard_map/ppermute | solution.py:384
  124.2 4.9 %collective-permute-start.7 = (bf16[384,128]{1,0:T(8,128)(2,1)}, bf16[384,128]{1,0:T(8,128)(2,1)}, u32[]{:S(2)}, u32[]{:S(2)}) collective-permute-start(bf16[384,128]{1,0:T(8,128)(2,1)} %get-tuple-element.23.refs_5_), channel_id=1, source_target_pairs={{0,112},{16,0},{32,16},{48,32},{64,48},{80,64},{96,80},{112,96},{1... | collective-permute-start | bytes 294920 | tf_op jit(solution)/shard_map/ppermute | solution.py:384
  129.2 6.7 %collective-permute-start.8 = (bf16[384,128]{1,0:T(8,128)(2,1)}, bf16[384,128]{1,0:T(8,128)(2,1)}, u32[]{:S(2)}, u32[]{:S(2)}) collective-permute-start(bf16[384,128]{1,0:T(8,128)(2,1)} %get-tuple-element.23.refs_5_), channel_id=1, source_target_pairs={{0,96},{16,112},{32,0},{48,16},{64,32},{80,48},{96,64},{112,80},{1... | collective-permute-start | bytes 294920 | tf_op jit(solution)/shard_map/ppermute | solution.py:384
  135.8 7.3 %collective-permute-start.9 = (bf16[384,128]{1,0:T(8,128)(2,1)}, bf16[384,128]{1,0:T(8,128)(2,1)}, u32[]{:S(2)}, u32[]{:S(2)}) collective-permute-start(bf16[384,128]{1,0:T(8,128)(2,1)} %get-tuple-element.23.refs_5_), channel_id=1, source_target_pairs={{0,80},{16,96},{32,112},{48,0},{64,16},{80,32},{96,48},{112,64},{1... | collective-permute-start | bytes 294920 | tf_op jit(solution)/shard_map/ppermute | solution.py:384
  143.1 1.7 collective-permute-start.20
  144.8 0.7 copy-start.6
  155.4 1.0 copy-start.2
  156.4 36.7 %copy-start.14 = (bf16[128,384]{1,0:T(8,128)(2,1)S(1)}, bf16[128,384]{1,0:T(8,128)(2,1)}, u32[]{:S(2)}) copy-start(bf16[128,384]{1,0:T(8,128)(2,1)} %get-tuple-element.42) | copy-start | bytes 294916
  156.4 36.7 %copy-start.15 = (bf16[128,384]{1,0:T(8,128)(2,1)S(1)}, bf16[128,384]{1,0:T(8,128)(2,1)}, u32[]{:S(2)}) copy-start(bf16[128,384]{1,0:T(8,128)(2,1)} %get-tuple-element.43) | copy-start | bytes 294916
  163.4 19.2 %collective-permute-start.21 = (bf16[400,128]{1,0:T(8,128)(2,1)}, bf16[400,128]{1,0:T(8,128)(2,1)S(1)}, u32[]{:S(2)}, u32[]{:S(2)}) collective-permute-start(bf16[400,128]{1,0:T(8,128)(2,1)} %get-tuple-element.35), channel_id=1, source_target_pairs={{0,64},{16,80},{32,96},{48,112},{64,0},{80,16},{96,32},{112,48},{1... | collective-permute-start | bytes 307208 | tf_op jit(solution)/shard_map/ppermute | solution.py:401
  170.0 14.0 %collective-permute-start.22 = (bf16[400,128]{1,0:T(8,128)(2,1)}, bf16[400,128]{1,0:T(8,128)(2,1)S(1)}, u32[]{:S(2)}, u32[]{:S(2)}) collective-permute-start(bf16[400,128]{1,0:T(8,128)(2,1)} %get-tuple-element.36), channel_id=1, source_target_pairs={{0,48},{16,64},{32,80},{48,96},{64,112},{80,0},{96,16},{112,32},{1... | collective-permute-start | bytes 307208 | tf_op jit(solution)/shard_map/ppermute | solution.py:401
  175.8 18.2 %collective-permute-start.23 = (bf16[400,128]{1,0:T(8,128)(2,1)}, bf16[400,128]{1,0:T(8,128)(2,1)S(1)}, u32[]{:S(2)}, u32[]{:S(2)}) collective-permute-start(bf16[400,128]{1,0:T(8,128)(2,1)} %get-tuple-element.37), channel_id=1, source_target_pairs={{0,80},{16,96},{32,112},{48,0},{64,16},{80,32},{96,48},{112,64},{1... | collective-permute-start | bytes 307208 | tf_op jit(solution)/shard_map/ppermute | solution.py:401
  175.8 18.2 %collective-permute-start.24 = (bf16[400,128]{1,0:T(8,128)(2,1)}, bf16[400,128]{1,0:T(8,128)(2,1)S(1)}, u32[]{:S(2)}, u32[]{:S(2)}) collective-permute-start(bf16[400,128]{1,0:T(8,128)(2,1)} %get-tuple-element.38), channel_id=1, source_target_pairs={{0,32},{16,48},{32,64},{48,80},{64,96},{80,112},{96,0},{112,16},{1... | collective-permute-start | bytes 307208 | tf_op jit(solution)/shard_map/ppermute | solution.py:401
  182.6 11.4 %collective-permute-start.25 = (bf16[400,128]{1,0:T(8,128)(2,1)}, bf16[400,128]{1,0:T(8,128)(2,1)S(1)}, u32[]{:S(2)}, u32[]{:S(2)}) collective-permute-start(bf16[400,128]{1,0:T(8,128)(2,1)} %get-tuple-element.39), channel_id=1, source_target_pairs={{0,96},{16,112},{32,0},{48,16},{64,32},{80,48},{96,64},{112,80},{1... | collective-permute-start | bytes 307208 | tf_op jit(solution)/shard_map/ppermute | solution.py:401
  182.6 13.0 %copy-start.7 = (bf16[400,128]{1,0:T(8,128)(2,1)}, bf16[400,128]{1,0:T(8,128)(2,1)S(1)}, u32[]{:S(2)}) copy-start(bf16[400,128]{1,0:T(8,128)(2,1)S(1)} %collective-permute-done.21.refs_1_) | copy-start | bytes 307204
  182.6 11.4 %collective-permute-start.26 = (bf16[400,128]{1,0:T(8,128)(2,1)}, bf16[400,128]{1,0:T(8,128)(2,1)S(1)}, u32[]{:S(2)}, u32[]{:S(2)}) collective-permute-start(bf16[400,128]{1,0:T(8,128)(2,1)} %get-tuple-element.40), channel_id=1, source_target_pairs={{0,16},{16,32},{32,48},{48,64},{64,80},{80,96},{96,112},{112,0},{1... | collective-permute-start | bytes 307208 | tf_op jit(solution)/shard_map/ppermute | solution.py:401
  184.0 11.7 %copy-start.8 = (bf16[400,128]{1,0:T(8,128)(2,1)}, bf16[400,128]{1,0:T(8,128)(2,1)S(1)}, u32[]{:S(2)}) copy-start(bf16[400,128]{1,0:T(8,128)(2,1)S(1)} %collective-permute-done.22.refs_2_) | copy-start | bytes 307204
  184.0 11.7 %collective-permute-start.27 = (bf16[400,128]{1,0:T(8,128)(2,1)}, bf16[400,128]{1,0:T(8,128)(2,1)S(1)}, u32[]{:S(2)}, u32[]{:S(2)}) collective-permute-start(bf16[400,128]{1,0:T(8,128)(2,1)} %get-tuple-element.41), channel_id=1, source_target_pairs={{0,112},{16,0},{32,16},{48,32},{64,48},{80,64},{96,80},{112,96},{1... | collective-permute-start | bytes 307208 | tf_op jit(solution)/shard_map/ppermute | solution.py:401
  194.0 1.7 copy-start.9
  194.0 1.7 copy-start.10
  194.0 1.6 copy-start.11
  194.0 1.6 copy-start.12
  195.7 0.6 copy-start.13
where the time goes:
time: 200 us; the launch traced here: 198 us
  waiting for transfers between devices  91.3 us (46%)
  starting transfers between devices  58.7 us (29%)
  Pallas kernels  40 us (20%)
  local copies, waits for them, and re-layouts  6.03 us (3%)
    ppermute x1, waiting for transfers between devices, layer(): f1 = lax.ppermute(features, 'yh', swap)  45.9 us
    ppermute x7, waiting for transfers between devices, layer(): qs[d] = lax.ppermute(q, 'z', ring(8, -d))  33.5 us
    ppermute x7, starting transfers between devices, layer(): got.append(lax.ppermute(parts[d], 'z', ring(8, d)))  29.4 us
    ppermute x7, starting transfers between devices, layer(): qs[d] = lax.ppermute(q, 'z', ring(8, -d))  18.1 us
    pallas_call x2, Pallas kernels, attn(): pl.pallas_call(functools.partial(attn_body, sets, bool(news), bool(prev))...  16.8 us
    pallas_call x2, Pallas kernels, prep(): pl.pallas_call(prep_body, grid=(HALF,), in_specs=[pl.BlockSpec((None, 128...  10.5 us
    pallas_call x1, Pallas kernels, layer(): pl.pallas_call(keyval_body, in_specs=[VM] * 3 + [HBM], out_specs=[VM, VM,...  6.02 us
    ppermute x1, waiting for transfers between devices, layer(): fm = lax.ppermute(both, 'x', ring(4, 2))  5.13 us
  transfers between devices with their start and end apart: 28, of which 14 were waited for; matrix products, arithmetic and copies ran while one was open for 2% of the time, Pallas kernels for 13%

commit v1 on v0

--- a/solution.py
+++ b/solution.py
@@ -22,7 +22,6 @@
 HD = 96
 HALF = 6
 WIN = ((0,), (0, 1), (1, 2), (2,))
-DIST = (4, 3, 5, 2, 6, 1, 7)
 
 
 def ring(n, k):
@@ -188,8 +187,8 @@
             for w, t in enumerate(WIN[h]):
                 rr = hrow[128 * t:128 * t + 128]
                 sel = (rr >= HD * h) & (rr < HD * h + HD)
-                block = q[128 * t:128 * t + 128].astype(F32)
-                qm[h, 128 * w:128 * w + 128] = jnp.where(sel, block, 0.0).astype(BF)
+                block = q[128 * t:128 * t + 128]
+                qm[h, 128 * w:128 * w + 128] = jnp.where(sel, block, jnp.zeros_like(block))
         cached = cnt[r]
         for i in range(len(new_refs)):
             @pl.when((nreq == r) & (npos[i] <= start + 256))
@@ -280,10 +279,8 @@
             o = o.astype(BF)
             oa[2 * pr, at] = o[:, :128]
             oa[2 * pr + 1, at] = o[:, 128:]
-            for term in terms:
-                part = lse.astype(BF).astype(F32)
+            for term, part in zip(terms, thirds(lse)):
                 term.append(part)
-                lse = lse - part
         rows = terms[0] + terms[1] + terms[2] + [jnp.zeros((4, 256), F32)]
         st = jnp.concatenate(rows, axis=0).astype(BF)
         oa[2 * pr, 384:400] = st[:, :128]
@@ -318,16 +315,15 @@
     )(lens, *metas, *qs, *kvs, *news, *prev)
 
 
-def combine_body(*refs):
-    o_ref = refs[-1]
-    parts = refs[:-1]
+def merged(parts):
     lses = []
     for p in parts:
         st = p[384:400].astype(F32)
         lses.append(st[0:4] + st[4:8] + st[8:12])
     top = functools.reduce(jnp.maximum, lses)
     ws = [jnp.exp(x - top) for x in lses]
-    inv = 1.0 / functools.reduce(jnp.add, ws)
+    total = functools.reduce(jnp.add, ws)
+    inv = 1.0 / total
     ws = [w * inv for w in ws]
     rows = []
     for h in range(4):
@@ -335,7 +331,28 @@
         for p, w in zip(parts, ws):
             acc = acc + p[HD * h:HD * h + HD].astype(F32) * w[h:h + 1]
         rows.append(acc)
-    o_ref[...] = jnp.concatenate(rows, axis=0).T.astype(BF)
+    return jnp.concatenate(rows, axis=0), top + jnp.log(total)
+
+
+def thirds(lse):
+    out = []
+    for _ in range(3):
+        part = lse.astype(BF).astype(F32)
+        out.append(part)
+        lse = lse - part
+    return out
+
+
+def merge_body(p2, r3, p6, r5, r4, m2, m6):
+    for parts, o_ref in (((p2, r3), m2), ((p6, r5, r4), m6)):
+        o, lse = merged(parts)
+        o_ref[0:384] = o.astype(BF)
+        o_ref[384:400] = jnp.concatenate(thirds(lse) + [jnp.zeros((4, 128), F32)], axis=0).astype(BF)
+
+
+def combine_body(*refs):
+    o, _ = merged(refs[:-1])
+    refs[-1][...] = o.T.astype(BF)
 
 
 def layer(features, gain, w_qkv, rope_factors, cache_len, cache_kv, block_owner, block_base):
@@ -364,7 +381,8 @@
     z = lax.axis_index("z")
     request = 2 * lax.axis_index("yl") + z // 4
     start = ((z % 4) * 2 + lax.axis_index("c")) * 128
-    positions = cache_len[request] + start + jnp.arange(128, dtype=I32)
+    length = jnp.sum(jnp.where(jnp.arange(4) == request, cache_len, 0))
+    positions = length + start + jnp.arange(128, dtype=I32)
     inv_freq = 1.0 / (rope_factors * jnp.power(10000.0, jnp.arange(48, dtype=F32) * 2.0 / HD))
     angles = inv_freq[:, None] * positions.astype(F32)[None, :]
     cos = jnp.cos(angles) * MSCALE
@@ -380,8 +398,10 @@
         name="query",
     )(gain.reshape(8, 1, 384), cos, sin, features, f1, fr, fl, fm, w)
     qs = [q] + [None] * 7
-    for d in DIST:
+    for d in (2, 6, 1, 7):
         qs[d] = lax.ppermute(q, "z", ring(8, -d))
+    for d, source, hop in ((4, 6, 2), (3, 2, -1), (5, 6, 1)):
+        qs[d] = lax.ppermute(qs[source], "z", ring(8, hop))
     new0, kn, vn = pl.pallas_call(
         keyval_body,
         in_specs=[VM] * 3 + [HBM],
@@ -396,16 +416,27 @@
     parts = attn(sets, cache_len, metas, qs, [kv0a, kv0b, kv1a, kv1b, kv2a, kv3a], [new0, new1])
     sets = ((2, HALF), (3, HALF))
     parts = attn(sets, cache_len, metas, qs, [kv2b, kv3b], prev=parts)
-    got = [parts[0]]
-    for d in DIST:
-        got.append(lax.ppermute(parts[d], "z", ring(8, d)))
+    r4 = lax.ppermute(parts[4], "z", ring(8, -2))
+    r3 = lax.ppermute(parts[3], "z", ring(8, 1))
+    r5 = lax.ppermute(parts[5], "z", ring(8, -1))
+    g1 = lax.ppermute(parts[1], "z", ring(8, 1))
+    g7 = lax.ppermute(parts[7], "z", ring(8, -1))
+    m2, m6 = pl.pallas_call(
+        merge_body,
+        in_specs=[VM] * 5,
+        out_specs=[VM] * 2,
+        out_shape=[S((400, 128), BF)] * 2,
+        name="merge",
+    )(parts[2], r3, parts[6], r5, r4)
+    g2 = lax.ppermute(m2, "z", ring(8, 2))
+    g6 = lax.ppermute(m6, "z", ring(8, -2))
     attended = pl.pallas_call(
         combine_body,
-        in_specs=[VM] * 8,
+        in_specs=[VM] * 5,
         out_specs=VM,
         out_shape=S((128, 384), BF),
         name="combine",
-    )(*got)
+    )(parts[0], g1, g7, g2, g6)
     return attended, new_kv
 
 

time: 200 us -> 191 us (0.955)
  starting transfers between devices: 58.7 us -> 46.5 us
  waiting for transfers between devices: 91.3 us -> 93.5 us
    ppermute x7 -> x10, waiting for transfers between devices: 1.88 us -> 20.9 us  [the longest x3 13.9 us: layer(): qs[d] = lax.ppermute(qs[source], 'z', ring(8, hop))]
    ppermute x7 -> x4, waiting for transfers between devices: 33.5 us -> 16.8 us  [layer(): qs[d] = lax.ppermute(q, 'z', ring(8, -d))]
    ppermute x7 -> x4, starting transfers between devices: 18.1 us -> 9.95 us  [layer(): qs[d] = lax.ppermute(q, 'z', ring(8, -d))]
    ppermute x7 -> x10, starting transfers between devices: 29.4 us -> 25.2 us  [the longest x1 9.6 us: layer(): r4 = lax.ppermute(parts[4], 'z', ring(8, -2))]
    unnamed x50 -> x54, local copies, waits for them, and re-layouts: 4.73 us -> 5.31 us
  transfers between devices with their start and end apart: 28 -> 28, of which waited for: 14 -> 15; matrix products, arithmetic and copies ran while one was open for 2% -> 2% of each run, Pallas kernels for 13% -> 14%
where the time goes in v1:
time: 191 us
  waiting for transfers between devices  93.5 us (49%)
  starting transfers between devices  46.5 us (24%)
  Pallas kernels  41.7 us (22%)
  local copies, waits for them, and re-layouts  5.96 us (3%)
    ppermute x1, waiting for transfers between devices, layer(): f1 = lax.ppermute(features, 'yh', swap)  45.8 us
    ppermute x4, waiting for transfers between devices, layer(): qs[d] = lax.ppermute(q, 'z', ring(8, -d))  16.8 us
    pallas_call x2, Pallas kernels, attn(): pl.pallas_call(functools.partial(attn_body, sets, bool(news), bool(prev))...  16.8 us
    ppermute x3, waiting for transfers between devices, layer(): qs[d] = lax.ppermute(qs[source], 'z', ring(8, hop))  13.9 us
    pallas_call x2, Pallas kernels, prep(): pl.pallas_call(prep_body, grid=(HALF,), in_specs=[pl.BlockSpec((None, 128...  10.5 us
    ppermute x4, starting transfers between devices, layer(): qs[d] = lax.ppermute(q, 'z', ring(8, -d))  9.95 us
    ppermute x1, starting transfers between devices, layer(): r4 = lax.ppermute(parts[4], 'z', ring(8, -2))  9.6 us
    pallas_call x1, Pallas kernels, layer(): pl.pallas_call(keyval_body, in_specs=[VM] * 3 + [HBM], out_specs=[VM, VM,...  6.03 us
  transfers between devices with their start and end apart: 28, of which 15 were waited for; matrix products, arithmetic and copies ran while one was open for 2% of the time, Pallas kernels for 14%

profile of v1, /device:TPU:2, one launch (start us, length us, event | category | flops | bytes accessed | tf_op | source)
XLA Modules:
  0.0 190.8 jit_solution(15265799562533054446)
XLA Ops:
  0.6 5.2 %prep.3.refs_13_ = bf16[6,768,128]{2,1,0:T(8,128)(2,1)} custom-call(bf16[12,128,2,384]{3,2,1,0:T(2,128)(2,1)} %kv_ref.3), custom_call_target="tpu_custom_call" | custom-call | tf_op jit(solution)/shard_map/prep/pallas_call | solution.py:47
  5.9 0.0 copy-start.22
  5.9 1.7 collective-permute-start.18
  7.6 5.3 %prep.2.refs_14_ = bf16[6,768,128]{2,1,0:T(8,128)(2,1)} custom-call(bf16[12,128,2,384]{3,2,1,0:T(2,128)(2,1)} %kv_ref.3), custom_call_target="tpu_custom_call" | custom-call | tf_op jit(solution)/shard_map/prep/pallas_call | solution.py:47
  12.8 0.4 collective-permute-start.14
  13.3 3.2 %collective-permute-start.3 = (bf16[128,384]{1,0:T(8,128)(2,1)S(1)}, bf16[128,384]{1,0:T(8,128)(2,1)S(1)}, u32[]{:S(2)}, u32[]{:S(2)}) collective-permute-start(bf16[128,384]{1,0:T(8,128)(2,1)S(1)} %copy-done.3), channel_id=1, source_target_pairs={{0,4},{4,0},{1,5},{5,1},{2,6},{6,2},{3,7},{7,3},{8,12},{12,8},{9,1... | collective-permute-start | bytes 294920 | tf_op jit(solution)/shard_map/ppermute | solution.py:361
  16.5 0.8 collective-permute-start.1
  17.3 0.7 constant_dynamic-update-slice_fusion.1
  17.9 45.8 %collective-permute-done.3.f1 = bf16[128,384]{1,0:T(8,128)(2,1)S(1)} collective-permute-done((bf16[128,384]{1,0:T(8,128)(2,1)S(1)}, bf16[128,384]{1,0:T(8,128)(2,1)S(1)}, u32[]{:S(2)}, u32[]{:S(2)}) %collective-permute-start.3) | collective-permute-done | bytes 98336 | tf_op jit(solution)/shard_map/ppermute | solution.py:361
  63.8 0.6 copy-done.4
  64.4 0.7 constant_dynamic-update-slice_fusion
  65.1 1.5 collective-permute-start.4
  66.6 0.6 collective-permute-start.5
  67.2 0.7 fusion.2
  68.5 0.5 collective-permute-done.refs_2_
  69.1 0.2 collective-permute-start.16
  69.2 1.7 collective-permute-done.4.fr
  70.9 0.0 collective-permute-done.18.refs_17_
  70.9 0.5 collective-permute-start.19
  71.5 0.2 copy-done.8
  71.6 0.0 collective-permute-done.14.refs_13_
  71.6 0.0 collective-permute-start.15
  71.6 1.0 collective-permute-done.5.fl
  72.6 2.3 %collective-permute-start.6 = (bf16[256,384]{1,0:T(8,128)(2,1)}, bf16[256,384]{1,0:T(8,128)(2,1)}, u32[]{:S(2)}, u32[]{:S(2)}) collective-permute-start(bf16[256,384]{1,0:T(8,128)(2,1)} %constant_dynamic-update-slice_fusion), channel_id=1, source_target_pairs={{0,2},{1,3},{2,0},{3,1},{4,6},{5,7},{6,4},{7,5},{8,10},{9,11},{10,... | collective-permute-start | bytes 589832 | tf_op jit(solution)/shard_map/ppermute | solution.py:365
  75.0 0.8 fusion.1
  75.8 5.0 %collective-permute-done.6.fm = bf16[256,384]{1,0:T(8,128)(2,1)} collective-permute-done((bf16[256,384]{1,0:T(8,128)(2,1)}, bf16[256,384]{1,0:T(8,128)(2,1)}, u32[]{:S(2)}, u32[]{:S(2)}) %collective-permute-start.6) | collective-permute-done | bytes 196640 | tf_op jit(solution)/shard_map/ppermute | solution.py:365
  80.8 0.0 collective-permute-start.2
  80.8 4.6 %query.1 = (bf16[384,128]{1,0:T(8,128)(2,1)}, bf16[8,128,384]{2,1,0:T(8,128)(2,1)}) custom-call(f32[8,1,384]{2,1,0:T(1,128)} %bitcast.10, f32[48,128]{1,0:T(8,128)} %get-tuple-element.51.cos_ref, f32[48,128]{1,0:T(8,128)} %get-tuple-element.50.sin_ref, bf16[128,384]{1,0:T(8,128)(2,1)} %f0.1, bf16[128,384]{1,0:T(8,128)(2,1)} %copy-done.4, ...), custom_call_target="tpu_custom_call" | custom-call | tf_op jit(solution)/shard_map/query/pallas_call | solution.py:392
  85.4 3.3 %collective-permute-start.10 = (bf16[384,128]{1,0:T(8,128)(2,1)}, bf16[384,128]{1,0:T(8,128)(2,1)}, u32[]{:S(2)}, u32[]{:S(2)}) collective-permute-start(bf16[384,128]{1,0:T(8,128)(2,1)} %get-tuple-element.25.refs_5_), channel_id=1, source_target_pairs={{0,32},{16,48},{32,64},{48,80},{64,96},{80,112},{96,0},{112,16},{1... | collective-permute-start | bytes 294920 | tf_op jit(solution)/shard_map/ppermute | solution.py:402
  88.7 7.4 %collective-permute-done.10.refs_11_ = bf16[384,128]{1,0:T(8,128)(2,1)} collective-permute-done((bf16[384,128]{1,0:T(8,128)(2,1)}, bf16[384,128]{1,0:T(8,128)(2,1)}, u32[]{:S(2)}, u32[]{:S(2)}) %collective-permute-start.10) | collective-permute-done | bytes 98336 | tf_op jit(solution)/shard_map/ppermute | solution.py:402
  96.1 4.2 %collective-permute-start.8 = (bf16[384,128]{1,0:T(8,128)(2,1)}, bf16[384,128]{1,0:T(8,128)(2,1)}, u32[]{:S(2)}, u32[]{:S(2)}) collective-permute-start(bf16[384,128]{1,0:T(8,128)(2,1)} %get-tuple-element.25.refs_5_), channel_id=1, source_target_pairs={{0,96},{16,112},{32,0},{48,16},{64,32},{80,48},{96,64},{112,80},{1... | collective-permute-start | bytes 294920 | tf_op jit(solution)/shard_map/ppermute | solution.py:402
  100.3 3.8 %collective-permute-done.8.refs_7_ = bf16[384,128]{1,0:T(8,128)(2,1)} collective-permute-done((bf16[384,128]{1,0:T(8,128)(2,1)}, bf16[384,128]{1,0:T(8,128)(2,1)}, u32[]{:S(2)}, u32[]{:S(2)}) %collective-permute-start.8) | collective-permute-done | bytes 98336 | tf_op jit(solution)/shard_map/ppermute | solution.py:402
  104.1 0.5 collective-permute-start.13
  104.6 5.6 %collective-permute-done.13.refs_12_ = bf16[384,128]{1,0:T(8,128)(2,1)} collective-permute-done((bf16[384,128]{1,0:T(8,128)(2,1)}, bf16[384,128]{1,0:T(8,128)(2,1)}, u32[]{:S(2)}, u32[]{:S(2)}) %collective-permute-start.13) | collective-permute-done | bytes 98336 | tf_op jit(solution)/shard_map/ppermute | solution.py:402
  110.3 1.9 collective-permute-start.7
  112.2 6.0 %keyval.1 = (bf16[768,128]{1,0:T(8,128)(2,1)}, bf16[128,384]{1,0:T(8,128)(2,1)}, bf16[128,384]{1,0:T(8,128)(2,1)}) custom-call(f32[48,128]{1,0:T(8,128)} %get-tuple-element.51.cos_ref, f32[48,128]{1,0:T(8,128)} %get-tuple-element.50.sin_ref, bf16[8,128,384]{2,1,0:T(8,128)(2,1)} %get-tuple-element.26.n_ref, bf16[3,3072,384]{2,1,0:T(8,128)(2,1)} %bitcast.7), custom_call_target="tpu_custom_call" | custom-call | tf_op jit(solution)/shard_map/keyval/pallas_call | solution.py:405
  118.2 0.0 collective-permute-done.7.refs_6_
  118.2 0.1 collective-permute-start.20
  118.3 1.8 collective-permute-done.20.refs_20_
  120.1 0.4 collective-permute-start.11
  120.5 6.8 %collective-permute-done.11.refs_9_ = bf16[384,128]{1,0:T(8,128)(2,1)S(1)} collective-permute-done((bf16[384,128]{1,0:T(8,128)(2,1)}, bf16[384,128]{1,0:T(8,128)(2,1)S(1)}, u32[]{:S(2)}, u32[]{:S(2)}) %collective-permute-start.11) | collective-permute-done | bytes 98336 | tf_op jit(solution)/shard_map/ppermute | solution.py:404
  127.3 2.1 %collective-permute-start.12 = (bf16[384,128]{1,0:T(8,128)(2,1)}, bf16[384,128]{1,0:T(8,128)(2,1)S(1)}, u32[]{:S(2)}, u32[]{:S(2)}) collective-permute-start(bf16[384,128]{1,0:T(8,128)(2,1)} %collective-permute-done.10.refs_11_), channel_id=1, source_target_pairs={{0,16},{16,32},{32,48},{48,64},{64,80},{80,96},{96,112},{112,0},{1... | collective-permute-start | bytes 294920 | tf_op jit(solution)/shard_map/ppermute | solution.py:404
  129.5 3.9 %collective-permute-done.12.refs_10_ = bf16[384,128]{1,0:T(8,128)(2,1)S(1)} collective-permute-done((bf16[384,128]{1,0:T(8,128)(2,1)}, bf16[384,128]{1,0:T(8,128)(2,1)S(1)}, u32[]{:S(2)}, u32[]{:S(2)}) %collective-permute-start.12) | collective-permute-done | bytes 98336 | tf_op jit(solution)/shard_map/ppermute | solution.py:404
  133.4 1.6 collective-permute-start.9
  135.0 3.2 %collective-permute-done.9.refs_8_ = bf16[384,128]{1,0:T(8,128)(2,1)S(1)} collective-permute-done((bf16[384,128]{1,0:T(8,128)(2,1)}, bf16[384,128]{1,0:T(8,128)(2,1)S(1)}, u32[]{:S(2)}, u32[]{:S(2)}) %collective-permute-start.9) | collective-permute-done | bytes 98336 | tf_op jit(solution)/shard_map/ppermute | solution.py:404
  138.2 0.6 copy-done.7
  138.9 0.0 collective-permute-done.19.refs_18_
  138.9 9.8 %attn.2 = (bf16[400,128]{1,0:T(8,128)(2,1)}, bf16[400,128]{1,0:T(8,128)(2,1)}, bf16[400,128]{1,0:T(8,128)(2,1)}, bf16[400,128]{1,0:T(8,128)(2,1)}, bf16[400,128]...) custom-call(s32[4]{0:T(128)} %refs_0_.3, s32[2,12]{1,0:T(2,128)} %copy-done.18, ...), custom_call_target="tpu_custom_call" | custom-call | tf_op jit(solution)/shard_map/attn/pallas_call | solution.py:297
  148.6 1.0 copy-done.2
  149.7 7.0 %attn.3 = (bf16[400,128]{1,0:T(8,128)(2,1)}, bf16[400,128]{1,0:T(8,128)(2,1)}, bf16[400,128]{1,0:T(8,128)(2,1)}, bf16[400,128]{1,0:T(8,128)(2,1)}, bf16[400,128]...) custom-call(s32[4]{0:T(128)} %refs_0_.3, s32[2,12]{1,0:T(2,128)} %copy-done.18, ...), custom_call_target="tpu_custom_call" | custom-call | tf_op jit(solution)/shard_map/attn/pallas_call | solution.py:297
  156.7 1.0 collective-permute-start.23
  157.7 2.3 %collective-permute-start.24 = (bf16[400,128]{1,0:T(8,128)(2,1)}, bf16[400,128]{1,0:T(8,128)(2,1)S(1)}, u32[]{:S(2)}, u32[]{:S(2)}) collective-permute-start(bf16[400,128]{1,0:T(8,128)(2,1)} %get-tuple-element.42), channel_id=1, source_target_pairs={{0,112},{16,0},{32,16},{48,32},{64,48},{80,64},{96,80},{112,96},{1... | collective-permute-start | bytes 307208 | tf_op jit(solution)/shard_map/ppermute | solution.py:421
  160.0 9.6 %collective-permute-start.25 = (bf16[400,128]{1,0:T(8,128)(2,1)}, bf16[400,128]{1,0:T(8,128)(2,1)S(1)}, u32[]{:S(2)}, u32[]{:S(2)}) collective-permute-start(bf16[400,128]{1,0:T(8,128)(2,1)} %get-tuple-element.43), channel_id=1, source_target_pairs={{0,96},{16,112},{32,0},{48,16},{64,32},{80,48},{96,64},{112,80},{1... | collective-permute-start | bytes 307208 | tf_op jit(solution)/shard_map/ppermute | solution.py:419
  169.6 0.1 collective-permute-start.21
  169.7 3.1 %collective-permute-start.22 = (bf16[400,128]{1,0:T(8,128)(2,1)}, bf16[400,128]{1,0:T(8,128)(2,1)S(1)}, u32[]{:S(2)}, u32[]{:S(2)}) collective-permute-start(bf16[400,128]{1,0:T(8,128)(2,1)} %get-tuple-element.38), channel_id=1, source_target_pairs={{0,112},{16,0},{32,16},{48,32},{64,48},{80,64},{96,80},{112,96},{1... | collective-permute-start | bytes 307208 | tf_op jit(solution)/shard_map/ppermute | solution.py:423
  172.9 1.4 collective-permute-done.25.r4
  174.2 0.6 copy-done.15
  174.9 1.9 merge.1
  176.7 4.9 %collective-permute-start.26 = (bf16[400,128]{1,0:T(8,128)(2,1)}, bf16[400,128]{1,0:T(8,128)(2,1)S(1)}, u32[]{:S(2)}, u32[]{:S(2)}) collective-permute-start(bf16[400,128]{1,0:T(8,128)(2,1)} %get-tuple-element.44), channel_id=1, source_target_pairs={{0,32},{16,48},{32,64},{48,80},{64,96},{80,112},{96,0},{112,16},{1... | collective-permute-start | bytes 307208 | tf_op jit(solution)/shard_map/ppermute | solution.py:431
  181.7 0.9 copy.10
  182.6 2.4 %collective-permute-done.26.refs_3_ = bf16[400,128]{1,0:T(8,128)(2,1)S(1)} collective-permute-done((bf16[400,128]{1,0:T(8,128)(2,1)}, bf16[400,128]{1,0:T(8,128)(2,1)S(1)}, u32[]{:S(2)}, u32[]{:S(2)}) %collective-permute-start.26) | collective-permute-done | bytes 102432 | tf_op jit(solution)/shard_map/ppermute | solution.py:431
  185.0 3.1 %collective-permute-done.27.refs_4_ = bf16[400,128]{1,0:T(8,128)(2,1)S(1)} collective-permute-done((bf16[400,128]{1,0:T(8,128)(2,1)}, bf16[400,128]{1,0:T(8,128)(2,1)S(1)}, u32[]{:S(2)}, u32[]{:S(2)}) %collective-permute-start.27) | collective-permute-done | bytes 102432 | tf_op jit(solution)/shard_map/ppermute | solution.py:432
  188.2 0.6 copy-done.12
  188.8 1.9 %combine.1 = bf16[128,384]{1,0:T(8,128)(2,1)} custom-call(bf16[400,128]{1,0:T(8,128)(2,1)} %get-tuple-element.36.refs_0_, bf16[400,128]{1,0:T(8,128)(2,1)} %copy-done.9, bf16[400,128]{1,0:T(8,128)(2,1)} %copy-done.10, bf16[400,128]{1,0:T(8,128)(2,1)} %copy-done.11, bf16[400,128]{1,0:T(8,128)(2,1)} %copy-done.12), custom_call_target="tpu_custom_call" | custom-call | tf_op jit(solution)/shard_map/combine/pallas_call | solution.py:433
  (61 shorter events, 0.2 us)
Async XLA Ops:
  5.9 7.4 %copy-start.3 = (bf16[128,384]{1,0:T(8,128)(2,1)S(1)}, bf16[128,384]{1,0:T(8,128)(2,1)}, u32[]{:S(2)}) copy-start(bf16[128,384]{1,0:T(8,128)(2,1)} %f0.1) | copy-start | bytes 294916
  5.9 10.6 %copy-start.23 = (s32[12]{0:T(128)S(1)}, s32[12]{0:T(128)}, u32[]{:S(2)}) copy-start(s32[12]{0:T(128)} %param.15) | copy-start | bytes 148
  5.9 10.6 %copy-start.24 = (s32[12]{0:T(128)S(1)}, s32[12]{0:T(128)}, u32[]{:S(2)}) copy-start(s32[12]{0:T(128)} %param.14) | copy-start | bytes 148
  5.9 60.7 %copy-start.25 = (f32[48]{0:T(128)S(1)}, f32[48]{0:T(128)}, u32[]{:S(2)}) copy-start(f32[48]{0:T(128)} %param.11) | copy-start | bytes 580
  5.9 61.3 %copy-start.22 = (s32[4]{0:T(128)S(1)}, s32[4]{0:T(128)}, u32[]{:S(2)}) copy-start(s32[4]{0:T(128)} %refs_0_.3) | copy-start | bytes 52
  5.9 63.2 %copy-start = (bf16[6,768,128]{2,1,0:T(8,128)(2,1)S(1)}, bf16[6,768,128]{2,1,0:T(8,128)(2,1)}, u32[]{:S(2)}) copy-start(bf16[6,768,128]{2,1,0:T(8,128)(2,1)} %prep.3.refs_13_) | copy-start | bytes 3538948
  5.9 65.0 %collective-permute-start.18 = (bf16[6,768,128]{2,1,0:T(8,128)(2,1)}, bf16[6,768,128]{2,1,0:T(8,128)(2,1)}, u32[]{:S(2)}, u32[]{:S(2)}) collective-permute-start(bf16[6,768,128]{2,1,0:T(8,128)(2,1)} %prep.3.refs_13_), channel_id=1, source_target_pairs={{0,128},{128,0},{1,129},{129,1},{2,130},{130,2},{3,131},{131,3},{4... | collective-permute-start | bytes 3538952 | tf_op jit(solution)/shard_map/ppermute | solution.py:363
  12.8 58.8 %collective-permute-start.14 = (bf16[6,768,128]{2,1,0:T(8,128)(2,1)}, bf16[6,768,128]{2,1,0:T(8,128)(2,1)S(1)}, u32[]{:S(2)}, u32[]{:S(2)}) collective-permute-start(bf16[6,768,128]{2,1,0:T(8,128)(2,1)} %prep.2.refs_14_), channel_id=1, source_target_pairs={{0,128},{128,0},{1,129},{129,1},{2,130},{130,2},{3,131},{131,3},{4... | collective-permute-start | bytes 3538952 | tf_op jit(solution)/shard_map/ppermute | solution.py:370
  13.3 50.5 %collective-permute-start.3 = (bf16[128,384]{1,0:T(8,128)(2,1)S(1)}, bf16[128,384]{1,0:T(8,128)(2,1)S(1)}, u32[]{:S(2)}, u32[]{:S(2)}) collective-permute-start(bf16[128,384]{1,0:T(8,128)(2,1)S(1)} %copy-done.3), channel_id=1, source_target_pairs={{0,4},{4,0},{1,5},{5,1},{2,6},{6,2},{3,7},{7,3},{8,12},{12,8},{9,1... | collective-permute-start | bytes 294920 | tf_op jit(solution)/shard_map/ppermute | solution.py:361
  16.5 68.8 %copy-start.18 = (s32[2,12]{1,0:T(2,128)}, s32[2,12]{1,0:T(2,128)S(1)}, u32[]{:S(2)}) copy-start(s32[2,12]{1,0:T(2,128)S(1)} %pad_add_fusion.refs_1_) | copy-start | bytes 292
  16.5 51.4 %collective-permute-start.1 = (s32[2,12]{1,0:T(2,128)S(1)}, s32[2,12]{1,0:T(2,128)S(1)}, u32[]{:S(2)}, u32[]{:S(2)}) collective-permute-start(s32[2,12]{1,0:T(2,128)S(1)} %pad_add_fusion.refs_1_), channel_id=1, source_target_pairs={{0,128},{128,0},{1,129},{129,1},{2,130},{130,2},{3,131},{131,3},{4... | collective-permute-start | bytes 296 | tf_op jit(solution)/shard_map/ppermute | solution.py:376
  63.8 0.6 copy-start.4
  65.1 5.9 %collective-permute-start.4 = (bf16[256,384]{1,0:T(8,128)(2,1)}, bf16[256,384]{1,0:T(8,128)(2,1)S(1)}, u32[]{:S(2)}, u32[]{:S(2)}) collective-permute-start(bf16[256,384]{1,0:T(8,128)(2,1)} %constant_dynamic-update-slice_fusion), channel_id=1, source_target_pairs={{0,1},{1,2},{2,3},{3,0},{4,5},{5,6},{6,7},{7,4},{8,9},{9,10},{10,1... | collective-permute-start | bytes 589832 | tf_op jit(solution)/shard_map/ppermute | solution.py:366
  66.6 6.1 %collective-permute-start.5 = (bf16[256,384]{1,0:T(8,128)(2,1)}, bf16[256,384]{1,0:T(8,128)(2,1)}, u32[]{:S(2)}, u32[]{:S(2)}) collective-permute-start(bf16[256,384]{1,0:T(8,128)(2,1)} %constant_dynamic-update-slice_fusion), channel_id=1, source_target_pairs={{0,3},{1,0},{2,1},{3,2},{4,7},{5,4},{6,5},{7,6},{8,11},{9,8},{10,9... | collective-permute-start | bytes 589832 | tf_op jit(solution)/shard_map/ppermute | solution.py:367
  67.9 17.4 %copy-start.19 = (s32[2,12]{1,0:T(2,128)}, s32[2,12]{1,0:T(2,128)S(1)}, u32[]{:S(2)}) copy-start(s32[2,12]{1,0:T(2,128)S(1)} %collective-permute-done.1.refs_3_) | copy-start | bytes 292
  67.9 1.2 collective-permute-start
  69.1 16.3 %copy-start.20 = (s32[2,12]{1,0:T(2,128)}, s32[2,12]{1,0:T(2,128)S(1)}, u32[]{:S(2)}) copy-start(s32[2,12]{1,0:T(2,128)S(1)} %collective-permute-done.refs_2_) | copy-start | bytes 292
  69.1 69.1 %collective-permute-start.16 = (bf16[6,768,128]{2,1,0:T(8,128)(2,1)S(1)}, bf16[6,768,128]{2,1,0:T(8,128)(2,1)}, u32[]{:S(2)}, u32[]{:S(2)}) collective-permute-start(bf16[6,768,128]{2,1,0:T(8,128)(2,1)S(1)} %copy-done), channel_id=1, source_target_pairs={{0,8},{8,0},{1,9},{9,1},{2,10},{10,2},{3,11},{11,3},{4,12},{12,4},... | collective-permute-start | bytes 3538952 | tf_op jit(solution)/shard_map/ppermute | solution.py:371
  70.9 0.7 copy-start.8
  70.9 67.3 %collective-permute-start.17 = (bf16[6,768,128]{2,1,0:T(8,128)(2,1)}, bf16[6,768,128]{2,1,0:T(8,128)(2,1)}, u32[]{:S(2)}, u32[]{:S(2)}) collective-permute-start(bf16[6,768,128]{2,1,0:T(8,128)(2,1)} %prep.2.refs_14_), channel_id=1, source_target_pairs={{0,8},{8,0},{1,9},{9,1},{2,10},{10,2},{3,11},{11,3},{4,12},{12,4},... | collective-permute-start | bytes 3538952 | tf_op jit(solution)/shard_map/ppermute | solution.py:372
  70.9 67.9 %collective-permute-start.19 = (bf16[6,768,128]{2,1,0:T(8,128)(2,1)}, bf16[6,768,128]{2,1,0:T(8,128)(2,1)}, u32[]{:S(2)}, u32[]{:S(2)}) collective-permute-start(bf16[6,768,128]{2,1,0:T(8,128)(2,1)} %collective-permute-done.18.refs_17_), channel_id=1, source_target_pairs={{0,8},{8,0},{1,9},{9,1},{2,10},{10,2},{3,11},{11,3},{4,12},{12,4},... | collective-permute-start | bytes 3538952 | tf_op jit(solution)/shard_map/ppermute | solution.py:373
  71.6 13.7 %copy-start.1 = (bf16[6,768,128]{2,1,0:T(8,128)(2,1)}, bf16[6,768,128]{2,1,0:T(8,128)(2,1)S(1)}, u32[]{:S(2)}) copy-start(bf16[6,768,128]{2,1,0:T(8,128)(2,1)S(1)} %collective-permute-done.14.refs_13_) | copy-start | bytes 3538948
  71.6 77.0 %collective-permute-start.15 = (bf16[6,768,128]{2,1,0:T(8,128)(2,1)S(1)}, bf16[6,768,128]{2,1,0:T(8,128)(2,1)S(1)}, u32[]{:S(2)}, u32[]{:S(2)}) collective-permute-start(bf16[6,768,128]{2,1,0:T(8,128)(2,1)S(1)} %collective-permute-done.14.refs_13_), channel_id=1, source_target_pairs={{0,8},{8,0},{1,9},{9,1},{2,10},{10,2},{3,11},{11,3},{4,12},{12,4},... | collective-permute-start | bytes 3538952 | tf_op jit(solution)/shard_map/ppermute | solution.py:374
  72.6 8.1 %collective-permute-start.6 = (bf16[256,384]{1,0:T(8,128)(2,1)}, bf16[256,384]{1,0:T(8,128)(2,1)}, u32[]{:S(2)}, u32[]{:S(2)}) collective-permute-start(bf16[256,384]{1,0:T(8,128)(2,1)} %constant_dynamic-update-slice_fusion), channel_id=1, source_target_pairs={{0,2},{1,3},{2,0},{3,1},{4,6},{5,7},{6,4},{7,5},{8,10},{9,11},{10,... | collective-permute-start | bytes 589832 | tf_op jit(solution)/shard_map/ppermute | solution.py:365
  80.8 4.6 %collective-permute-start.2 = (s32[2,12]{1,0:T(2,128)S(1)}, s32[2,12]{1,0:T(2,128)S(1)}, u32[]{:S(2)}, u32[]{:S(2)}) collective-permute-start(s32[2,12]{1,0:T(2,128)S(1)} %collective-permute-done.1.refs_3_), channel_id=1, source_target_pairs={{0,8},{8,0},{1,9},{9,1},{2,10},{10,2},{3,11},{11,3},{4,12},{12,4},... | collective-permute-start | bytes 296 | tf_op jit(solution)/shard_map/ppermute | solution.py:378
  85.4 32.8 %copy-start.21 = (s32[2,12]{1,0:T(2,128)}, s32[2,12]{1,0:T(2,128)S(1)}, u32[]{:S(2)}) copy-start(s32[2,12]{1,0:T(2,128)S(1)} %collective-permute-done.2.refs_4_) | copy-start | bytes 292
  85.4 10.7 %collective-permute-start.10 = (bf16[384,128]{1,0:T(8,128)(2,1)}, bf16[384,128]{1,0:T(8,128)(2,1)}, u32[]{:S(2)}, u32[]{:S(2)}) collective-permute-start(bf16[384,128]{1,0:T(8,128)(2,1)} %get-tuple-element.25.refs_5_), channel_id=1, source_target_pairs={{0,32},{16,48},{32,64},{48,80},{64,96},{80,112},{96,0},{112,16},{1... | collective-permute-start | bytes 294920 | tf_op jit(solution)/shard_map/ppermute | solution.py:402
  96.1 8.0 %collective-permute-start.8 = (bf16[384,128]{1,0:T(8,128)(2,1)}, bf16[384,128]{1,0:T(8,128)(2,1)}, u32[]{:S(2)}, u32[]{:S(2)}) collective-permute-start(bf16[384,128]{1,0:T(8,128)(2,1)} %get-tuple-element.25.refs_5_), channel_id=1, source_target_pairs={{0,96},{16,112},{32,0},{48,16},{64,32},{80,48},{96,64},{112,80},{1... | collective-permute-start | bytes 294920 | tf_op jit(solution)/shard_map/ppermute | solution.py:402
  104.1 6.1 %collective-permute-start.13 = (bf16[384,128]{1,0:T(8,128)(2,1)}, bf16[384,128]{1,0:T(8,128)(2,1)}, u32[]{:S(2)}, u32[]{:S(2)}) collective-permute-start(bf16[384,128]{1,0:T(8,128)(2,1)} %get-tuple-element.25.refs_5_), channel_id=1, source_target_pairs={{0,16},{16,32},{32,48},{48,64},{64,80},{80,96},{96,112},{112,0},{1... | collective-permute-start | bytes 294920 | tf_op jit(solution)/shard_map/ppermute | solution.py:402
  110.3 7.9 %collective-permute-start.7 = (bf16[384,128]{1,0:T(8,128)(2,1)}, bf16[384,128]{1,0:T(8,128)(2,1)}, u32[]{:S(2)}, u32[]{:S(2)}) collective-permute-start(bf16[384,128]{1,0:T(8,128)(2,1)} %get-tuple-element.25.refs_5_), channel_id=1, source_target_pairs={{0,112},{16,0},{32,16},{48,32},{64,48},{80,64},{96,80},{112,96},{1... | collective-permute-start | bytes 294920 | tf_op jit(solution)/shard_map/ppermute | solution.py:402
  118.2 1.9 collective-permute-start.20
  120.1 7.3 %collective-permute-start.11 = (bf16[384,128]{1,0:T(8,128)(2,1)}, bf16[384,128]{1,0:T(8,128)(2,1)S(1)}, u32[]{:S(2)}, u32[]{:S(2)}) collective-permute-start(bf16[384,128]{1,0:T(8,128)(2,1)} %collective-permute-done.10.refs_11_), channel_id=1, source_target_pairs={{0,32},{16,48},{32,64},{48,80},{64,96},{80,112},{96,0},{112,16},{1... | collective-permute-start | bytes 294920 | tf_op jit(solution)/shard_map/ppermute | solution.py:404
  127.3 10.9 %copy-start.5 = (bf16[384,128]{1,0:T(8,128)(2,1)}, bf16[384,128]{1,0:T(8,128)(2,1)S(1)}, u32[]{:S(2)}) copy-start(bf16[384,128]{1,0:T(8,128)(2,1)S(1)} %collective-permute-done.11.refs_9_) | copy-start | bytes 294916
  127.3 6.0 %collective-permute-start.12 = (bf16[384,128]{1,0:T(8,128)(2,1)}, bf16[384,128]{1,0:T(8,128)(2,1)S(1)}, u32[]{:S(2)}, u32[]{:S(2)}) collective-permute-start(bf16[384,128]{1,0:T(8,128)(2,1)} %collective-permute-done.10.refs_11_), channel_id=1, source_target_pairs={{0,16},{16,32},{32,48},{48,64},{64,80},{80,96},{96,112},{112,0},{1... | collective-permute-start | bytes 294920 | tf_op jit(solution)/shard_map/ppermute | solution.py:404
  133.4 4.9 %copy-start.6 = (bf16[384,128]{1,0:T(8,128)(2,1)}, bf16[384,128]{1,0:T(8,128)(2,1)S(1)}, u32[]{:S(2)}) copy-start(bf16[384,128]{1,0:T(8,128)(2,1)S(1)} %collective-permute-done.12.refs_10_) | copy-start | bytes 294916
  133.4 4.8 %collective-permute-start.9 = (bf16[384,128]{1,0:T(8,128)(2,1)}, bf16[384,128]{1,0:T(8,128)(2,1)S(1)}, u32[]{:S(2)}, u32[]{:S(2)}) collective-permute-start(bf16[384,128]{1,0:T(8,128)(2,1)} %collective-permute-done.8.refs_7_), channel_id=1, source_target_pairs={{0,112},{16,0},{32,16},{48,32},{64,48},{80,64},{96,80},{112,96},{1... | collective-permute-start | bytes 294920 | tf_op jit(solution)/shard_map/ppermute | solution.py:404
  138.2 0.6 copy-start.7
  148.6 1.0 copy-start.2
  149.7 32.0 %copy-start.16 = (bf16[128,384]{1,0:T(8,128)(2,1)S(1)}, bf16[128,384]{1,0:T(8,128)(2,1)}, u32[]{:S(2)}) copy-start(bf16[128,384]{1,0:T(8,128)(2,1)} %get-tuple-element.46) | copy-start | bytes 294916
  149.7 32.0 %copy-start.17 = (bf16[128,384]{1,0:T(8,128)(2,1)S(1)}, bf16[128,384]{1,0:T(8,128)(2,1)}, u32[]{:S(2)}) copy-start(bf16[128,384]{1,0:T(8,128)(2,1)} %get-tuple-element.47) | copy-start | bytes 294916
  156.7 16.2 %collective-permute-start.23 = (bf16[400,128]{1,0:T(8,128)(2,1)}, bf16[400,128]{1,0:T(8,128)(2,1)S(1)}, u32[]{:S(2)}, u32[]{:S(2)}) collective-permute-start(bf16[400,128]{1,0:T(8,128)(2,1)} %get-tuple-element.40), channel_id=1, source_target_pairs={{0,16},{16,32},{32,48},{48,64},{64,80},{80,96},{96,112},{112,0},{1... | collective-permute-start | bytes 307208 | tf_op jit(solution)/shard_map/ppermute | solution.py:420
  157.7 15.2 %collective-permute-start.24 = (bf16[400,128]{1,0:T(8,128)(2,1)}, bf16[400,128]{1,0:T(8,128)(2,1)S(1)}, u32[]{:S(2)}, u32[]{:S(2)}) collective-permute-start(bf16[400,128]{1,0:T(8,128)(2,1)} %get-tuple-element.42), channel_id=1, source_target_pairs={{0,112},{16,0},{32,16},{48,32},{64,48},{80,64},{96,80},{112,96},{1... | collective-permute-start | bytes 307208 | tf_op jit(solution)/shard_map/ppermute | solution.py:421
  160.0 14.2 %collective-permute-start.25 = (bf16[400,128]{1,0:T(8,128)(2,1)}, bf16[400,128]{1,0:T(8,128)(2,1)S(1)}, u32[]{:S(2)}, u32[]{:S(2)}) collective-permute-start(bf16[400,128]{1,0:T(8,128)(2,1)} %get-tuple-element.43), channel_id=1, source_target_pairs={{0,96},{16,112},{32,0},{48,16},{64,32},{80,48},{96,64},{112,80},{1... | collective-permute-start | bytes 307208 | tf_op jit(solution)/shard_map/ppermute | solution.py:419
  169.6 13.0 %collective-permute-start.21 = (bf16[400,128]{1,0:T(8,128)(2,1)}, bf16[400,128]{1,0:T(8,128)(2,1)S(1)}, u32[]{:S(2)}, u32[]{:S(2)}) collective-permute-start(bf16[400,128]{1,0:T(8,128)(2,1)} %get-tuple-element.37), channel_id=1, source_target_pairs={{0,16},{16,32},{32,48},{48,64},{64,80},{80,96},{96,112},{112,0},{1... | collective-permute-start | bytes 307208 | tf_op jit(solution)/shard_map/ppermute | solution.py:422
  169.7 12.9 %collective-permute-start.22 = (bf16[400,128]{1,0:T(8,128)(2,1)}, bf16[400,128]{1,0:T(8,128)(2,1)S(1)}, u32[]{:S(2)}, u32[]{:S(2)}) collective-permute-start(bf16[400,128]{1,0:T(8,128)(2,1)} %get-tuple-element.38), channel_id=1, source_target_pairs={{0,112},{16,0},{32,16},{48,32},{64,48},{80,64},{96,80},{112,96},{1... | collective-permute-start | bytes 307208 | tf_op jit(solution)/shard_map/ppermute | solution.py:423
  172.9 1.4 copy-start.13
  172.9 1.4 copy-start.14
  174.2 0.6 copy-start.15
  176.7 8.3 %collective-permute-start.26 = (bf16[400,128]{1,0:T(8,128)(2,1)}, bf16[400,128]{1,0:T(8,128)(2,1)S(1)}, u32[]{:S(2)}, u32[]{:S(2)}) collective-permute-start(bf16[400,128]{1,0:T(8,128)(2,1)} %get-tuple-element.44), channel_id=1, source_target_pairs={{0,32},{16,48},{32,64},{48,80},{64,96},{80,112},{96,0},{112,16},{1... | collective-permute-start | bytes 307208 | tf_op jit(solution)/shard_map/ppermute | solution.py:431
  181.6 6.5 %collective-permute-start.27 = (bf16[400,128]{1,0:T(8,128)(2,1)}, bf16[400,128]{1,0:T(8,128)(2,1)S(1)}, u32[]{:S(2)}, u32[]{:S(2)}) collective-permute-start(bf16[400,128]{1,0:T(8,128)(2,1)} %get-tuple-element.45), channel_id=1, source_target_pairs={{0,96},{16,112},{32,0},{48,16},{64,32},{80,48},{96,64},{112,80},{1... | collective-permute-start | bytes 307208 | tf_op jit(solution)/shard_map/ppermute | solution.py:432
  182.6 5.6 %copy-start.9 = (bf16[400,128]{1,0:T(8,128)(2,1)}, bf16[400,128]{1,0:T(8,128)(2,1)S(1)}, u32[]{:S(2)}) copy-start(bf16[400,128]{1,0:T(8,128)(2,1)S(1)} %collective-permute-done.21.refs_1_) | copy-start | bytes 307204
  182.6 5.6 %copy-start.10 = (bf16[400,128]{1,0:T(8,128)(2,1)}, bf16[400,128]{1,0:T(8,128)(2,1)S(1)}, u32[]{:S(2)}) copy-start(bf16[400,128]{1,0:T(8,128)(2,1)S(1)} %collective-permute-done.22.refs_2_) | copy-start | bytes 307204
  185.0 3.2 %copy-start.11 = (bf16[400,128]{1,0:T(8,128)(2,1)}, bf16[400,128]{1,0:T(8,128)(2,1)S(1)}, u32[]{:S(2)}) copy-start(bf16[400,128]{1,0:T(8,128)(2,1)S(1)} %collective-permute-done.26.refs_3_) | copy-start | bytes 307204
  188.2 0.7 copy-start.12
